TPU v7x, 32 devices: a whole 2x2x4 slice. The times are simulated.
32 devices in a mesh: seq: 8 (over y, x, core), heads: 4 (over z).
Axes of the slice: x: 2, y: 2, z: 4, core: 2. Of those that a mesh axis runs over, the one named last changes fastest.
Arguments:
- tokens: bfloat16 [8192, 768], P('seq'), may hold values from -6 to 6
- docs: int32 [8192], replicated, may hold values from 0 to 2, never falling along the last dimension, each value on 1 to 6144 neighbouring positions
- ln_gain: float32 [1, 2, 768], replicated, may hold values from 0.25 to 1.75
- ln_bias: float32 [1, 2, 768], replicated, may hold values from -1.75 to 1.75
- w_qkv: bfloat16 [1, 768, 3, 768], P(None, None, None, 'heads'), may hold values from -0.3125 to 0.3125
- b_qv: float32 [1, 2, 768], P(None, None, 'heads'), may hold values from -3 to 3
- w_out: bfloat16 [1, 768, 768], P(None, 'heads'), may hold values from -0.625 to 0.625
- b_out: float32 [1, 768], replicated, may hold values from -3 to 3
- w_up: bfloat16 [1, 768, 3072], P(None, None, 'heads'), may hold values from -0.21875 to 0.21875
- b_up: float32 [1, 3072], P(None, 'heads'), may hold values from -3 to 3
- w_down: bfloat16 [1, 3072, 768], P(None, 'heads'), may hold values from -0.15625 to 0.15625
- b_down: float32 [1, 768], replicated, may hold values from -3 to 3
- cotangent: bfloat16 [8192, 768], P('seq'), may hold values from -6 to 6
Outputs:
- output: bfloat16 [8192, 768], P('seq')
- grad_tokens: float32 [8192, 768], P('seq')
- grad_ln_gain: float32 [1, 2, 768], replicated
- grad_ln_bias: float32 [1, 2, 768], replicated
- grad_w_qkv: float32 [1, 768, 3, 768], P(None, None, None, 'heads')
- grad_b_qv: float32 [1, 2, 768], P(None, None, 'heads')
- grad_w_out: float32 [1, 768, 768], P(None, 'heads')
- grad_b_out: float32 [1, 768], replicated
- grad_w_up: float32 [1, 768, 3072], P(None, None, 'heads')
- grad_b_up: float32 [1, 3072], P(None, 'heads')
- grad_w_down: float32 [1, 3072, 768], P(None, 'heads')
- grad_b_down: float32 [1, 768], replicated
Inputs may be any that keep to these rules, and one draw needn't show every extreme that they name: `docs`: slide ids never fall along the sequence; each of the 3 slides holds 1 to 6144 tiles, and one holds exactly 6144.
All inputs are finite; a program needn't handle non-finite values.
Results may differ from a plain program's by a relative error of at most 0.025.
Values may be sent and summed in bfloat16 or wider, within the bound.
No kernel may reach another device: no remote copies, remote signals or barrier semaphores. Data moves between devices by JAX's collectives and lax.ppermute only.
A program may use at most 192 MiB of HBM per device.

v0:
```python
import jax
import jax.numpy as jnp
from jax import lax
from jax.sharding import PartitionSpec as P

HEAD_DIM = 48
LAYERS = 1
BRANCHES = 5


NEGATIVE = -1e30
epsilon = 1e-05


def swapped(array, axis, bit):
    return lax.ppermute(array, axis, [(i, i ^ 1 << bit) for i in range(lax.axis_size(axis))])


def norm_rows(values, gain_row, shift_row):
    center = values - jnp.mean(values, axis=-1, keepdims=True)
    spread = jnp.mean(center * center, axis=-1, keepdims=True)
    return center * lax.rsqrt(spread + epsilon) * gain_row + shift_row


def gelu_exact(values):
    return jax.nn.gelu(values, approximate=False)


def select_rows(values, pick_float):
    dilation = pick_float.shape[0]
    if dilation == 1:
        return values
    shaped = values.reshape(values.shape[0] // dilation, dilation, values.shape[1], values.shape[2])
    if values.dtype == jnp.bfloat16:
        return jnp.einsum(
            "nrhe,rh->nhe",
            shaped,
            pick_float.astype(jnp.bfloat16),
            preferred_element_type=jnp.float32,
        ).astype(jnp.bfloat16)
    return jnp.einsum("nrhe,rh->nhe", shaped, pick_float, precision=lax.Precision.HIGHEST)


def select_stat(values, pick_float):
    dilation = pick_float.shape[0]
    if dilation == 1:
        return values
    return jnp.sum(
        values.reshape(values.shape[0] // dilation, dilation, values.shape[1]) * pick_float[None],
        axis=1,
    )


def select_ids(id_rows, pick_int):
    dilation = pick_int.shape[0]
    return jnp.sum(
        id_rows.reshape(id_rows.shape[0] // dilation, dilation)[:, :, None] * pick_int[None], axis=1
    )


def place_rows(values, pick_float):
    if pick_float.shape[0] == 1:
        return values
    return (values[:, None] * pick_float[None, :, :, None]).reshape(
        -1, values.shape[1], values.shape[2]
    )


def place_stat(values, pick_float, fill_value):
    if pick_float.shape[0] == 1:
        return values
    return jnp.where(pick_float[None] > 0, values[:, None, :], fill_value).reshape(
        -1, values.shape[1]
    )


def join_pair(own_pair, their_pair, upper):
    return tuple(
        (
            jnp.where(
                upper,
                jnp.concatenate([their_block, own_block], 0),
                jnp.concatenate([own_block, their_block], 0),
            )
            for own_block, their_block in zip(own_pair, their_pair)
        )
    )


def split_pair(pair_rows, upper):
    half_rows = pair_rows[0].shape[0] // 2
    keep_part = tuple(
        (
            jnp.where(upper, block_rows[half_rows:], block_rows[:half_rows])
            for block_rows in pair_rows
        )
    )
    give_part = tuple(
        (
            jnp.where(upper, block_rows[:half_rows], block_rows[half_rows:])
            for block_rows in pair_rows
        )
    )
    return (keep_part, give_part)


def attend_forward(queries, key_rows, value_rows, query_ids, key_ids, scale):
    scores = (
        jnp.einsum("qhe,khe->hqk", queries, key_rows, preferred_element_type=jnp.float32) * scale
    )
    allowed = query_ids.T[:, :, None] == key_ids.T[:, None, :]
    row_peak = jnp.max(jnp.where(allowed, scores, NEGATIVE), axis=-1)
    prob_rows = jnp.where(allowed, jnp.exp(scores - row_peak[..., None]), 0.0)
    row_total = jnp.sum(prob_rows, axis=-1)
    summed = jnp.einsum(
        "hqk,khe->qhe",
        prob_rows.astype(jnp.bfloat16),
        value_rows,
        preferred_element_type=jnp.float32,
    )
    return (summed, row_peak.T, row_total.T)


def attend_backward(
    queries, key_rows, value_rows, query_ids, key_ids, row_peak, grad_summed, grad_total, scale
):
    scores = (
        jnp.einsum("qhe,khe->hqk", queries, key_rows, preferred_element_type=jnp.float32) * scale
    )
    allowed = query_ids.T[:, :, None] == key_ids.T[:, None, :]
    prob_rows = jnp.where(allowed, jnp.exp(scores - row_peak.T[..., None]), 0.0)
    grad_prob = jnp.einsum(
        "qhe,khe->hqk", grad_summed, value_rows, preferred_element_type=jnp.float32
    )
    grad_score = (prob_rows * (grad_prob + grad_total.T[..., None])).astype(jnp.bfloat16)
    grad_query = (
        jnp.einsum("hqk,khe->qhe", grad_score, key_rows, preferred_element_type=jnp.float32) * scale
    )
    grad_key = (
        jnp.einsum("hqk,qhe->khe", grad_score, queries, preferred_element_type=jnp.float32) * scale
    )
    grad_value = jnp.einsum(
        "hqk,qhe->khe",
        prob_rows.astype(jnp.bfloat16),
        grad_summed,
        preferred_element_type=jnp.float32,
    )
    return (grad_query, grad_key, grad_value)


def shards(
    tokens, docs, ln_gain, ln_bias, w_qkv, b_qv, w_out, b_out, w_up, b_up, w_down, b_down, cotangent
):
    rows = tokens.shape[0]
    feat_here = w_qkv.shape[3]
    heads_here = feat_here // HEAD_DIM
    head_shape = (rows, heads_here, HEAD_DIM)
    seq_count = lax.axis_size("seq")
    seq_bits = seq_count.bit_length() - 1
    seq_pos = lax.axis_index("seq")
    head_pos = lax.axis_index("heads")
    scale = HEAD_DIM ** (-0.5)
    head_ids = head_pos * heads_here + jnp.arange(heads_here, dtype=jnp.int32)
    own_ids = lax.dynamic_slice_in_dim(docs, seq_pos * rows, rows)
    branch_items = []
    for branch_index in range(BRANCHES):
        dilation = 2**branch_index
        group_bits = min(branch_index, seq_bits)
        group_size = 2**group_bits
        pick_int = (
            jnp.arange(dilation, dtype=jnp.int32)[:, None] == head_ids[None, :] % dilation
        ).astype(jnp.int32)
        pick_float = pick_int.astype(jnp.float32)
        query_ids = select_ids(own_ids, pick_int)
        group_docs = lax.dynamic_slice_in_dim(
            docs, seq_pos // group_size * (group_size * rows), group_size * rows
        )
        key_ids = select_ids(group_docs, pick_int)
        branch_items.append((pick_float, group_bits, query_ids, key_ids))

    def reduce_heads(left, weight, form):
        return lax.psum(jnp.einsum(form, left, weight, preferred_element_type=jnp.float32), "heads")

    def join_heads(share, weight, form):
        return (share, jnp.einsum(form, share, weight, preferred_element_type=jnp.float32))

    current = tokens.astype(jnp.float32)
    grad_running = cotangent.astype(jnp.float32)
    layer_index = 0
    gains = ln_gain[layer_index]
    shifts = ln_bias[layer_index]
    normed_share = norm_rows(current, gains[0], shifts[0]).astype(jnp.bfloat16)
    normed_b, projected = join_heads(normed_share, w_qkv[layer_index], "td,dcf->tcf")
    queries = (projected[:, 0] + b_qv[layer_index, 0]).astype(jnp.bfloat16).reshape(head_shape)
    key_rows = projected[:, 1].astype(jnp.bfloat16).reshape(head_shape)
    value_rows = (projected[:, 2] + b_qv[layer_index, 1]).astype(jnp.bfloat16).reshape(head_shape)
    local_sets = [
        (select_rows(key_rows, branch_item[0]), select_rows(value_rows, branch_item[0]))
        for branch_item in branch_items
    ]
    gathered = list(local_sets)
    for spread_branch_index in range(1, BRANCHES):
        for bit_index in range(branch_items[spread_branch_index][1]):
            upper = seq_pos // (1 << bit_index) % 2 == 1
            spread_current = gathered[spread_branch_index]
            received = swapped((spread_current[0], spread_current[1]), "seq", bit_index)
            gathered[spread_branch_index] = join_pair(spread_current, received, upper)
    query_sets = [select_rows(queries, branch_item[0]) for branch_item in branch_items]
    peak_sets = []
    placed = []
    for branch_index in range(BRANCHES):
        pick_float, group_bits, query_ids, key_ids = branch_items[branch_index]
        summed, row_peak, row_total = attend_forward(
            query_sets[branch_index],
            gathered[branch_index][0],
            gathered[branch_index][1],
            query_ids,
            key_ids,
            scale,
        )
        peak_sets.append(row_peak)
        placed.append(
            (
                place_rows(summed, pick_float),
                place_stat(row_peak, pick_float, NEGATIVE),
                place_stat(row_total, pick_float, 0.0),
            )
        )
    row_top = placed[0][1]
    for placed_item in placed[1:]:
        row_top = jnp.maximum(row_top, placed_item[1])
    factors = [jnp.exp(placed_item[1] - row_top) for placed_item in placed]
    denominator = jnp.zeros_like(row_top)
    numerator = jnp.zeros(head_shape, jnp.float32)
    for factor_row, placed_item in zip(factors, placed):
        denominator = denominator + factor_row * placed_item[2]
        numerator = numerator + factor_row[..., None] * placed_item[0]
    merged = numerator / denominator[..., None]
    shares = [factor_row / denominator for factor_row in factors]
    attn_b = merged.reshape(rows, feat_here).astype(jnp.bfloat16)
    residual = current + reduce_heads(attn_b, w_out[layer_index], "tf,fd->td") + b_out[layer_index]
    normed_two_share = norm_rows(residual, gains[1], shifts[1]).astype(jnp.bfloat16)
    normed_two, up_term = join_heads(normed_two_share, w_up[layer_index], "td,df->tf")
    pre_act = up_term + b_up[layer_index]
    activated = gelu_exact(pre_act).astype(jnp.bfloat16)
    layer_out = (
        residual + reduce_heads(activated, w_down[layer_index], "tf,fd->td") + b_down[layer_index]
    )
    kept_state = (
        current,
        normed_b,
        queries,
        key_rows,
        value_rows,
        query_sets,
        gathered,
        peak_sets,
        shares,
        merged,
        attn_b,
        residual,
        normed_two,
        pre_act,
        activated,
    )
    current, kept_state = (layer_out, kept_state)
    kept_layers = [kept_state]
    layer_terms = [None] * LAYERS
    for layer_index in reversed(range(LAYERS)):
        layer_kept_state = kept_layers[layer_index]
        (
            layer_current,
            layer_normed_b,
            layer_queries,
            layer_key_rows,
            layer_value_rows,
            layer_query_sets,
            layer_gathered,
            layer_peak_sets,
            layer_shares,
            layer_merged,
            layer_attn_b,
            layer_residual,
            layer_normed_two,
            layer_pre_act,
            layer_activated,
        ) = layer_kept_state
        layer_gains = ln_gain[layer_index]
        layer_shifts = ln_bias[layer_index]
        grad_down_bias = jnp.sum(grad_running, axis=0)
        grad_out_b = grad_running.astype(jnp.bfloat16)
        grad_out_full, grad_act = join_heads(grad_out_b, w_down[layer_index], "td,fd->tf")
        grad_down = jnp.einsum(
            "tf,td->fd", layer_activated, grad_out_full, preferred_element_type=jnp.float32
        )
        gelu_pull = jax.vjp(gelu_exact, layer_pre_act)[1]
        grad_pre = gelu_pull(grad_act)[0].astype(jnp.bfloat16)
        grad_up_bias = jnp.sum(grad_pre.astype(jnp.float32), axis=0)
        grad_up = jnp.einsum(
            "td,tf->df", layer_normed_two, grad_pre, preferred_element_type=jnp.float32
        )
        grad_normed_two = reduce_heads(grad_pre, w_up[layer_index], "tf,df->td")
        norm_pull_two = jax.vjp(norm_rows, layer_residual, layer_gains[1], layer_shifts[1])[1]
        grad_resid_norm, grad_gain_two, grad_shift_two = norm_pull_two(grad_normed_two)
        grad_resid = grad_running + grad_resid_norm
        grad_out_bias = jnp.sum(grad_resid, axis=0)
        grad_resid_b = grad_resid.astype(jnp.bfloat16)
        grad_resid_full, grad_merged_flat = join_heads(
            grad_resid_b, w_out[layer_index], "td,fd->tf"
        )
        grad_out_weight = jnp.einsum(
            "tf,td->fd", layer_attn_b, grad_resid_full, preferred_element_type=jnp.float32
        )
        grad_merged = grad_merged_flat.reshape(head_shape)
        delta_rows = jnp.sum(grad_merged * layer_merged, axis=-1)
        branch_grads = []
        for layer_branch_index in range(BRANCHES):
            layer_pick_float, layer_group_bits, layer_query_ids, layer_key_ids = branch_items[
                layer_branch_index
            ]
            grad_summed = select_rows(
                layer_shares[layer_branch_index][..., None] * grad_merged, layer_pick_float
            ).astype(jnp.bfloat16)
            grad_total = select_stat(
                -layer_shares[layer_branch_index] * delta_rows, layer_pick_float
            )
            branch_grads.append(
                attend_backward(
                    layer_query_sets[layer_branch_index],
                    layer_gathered[layer_branch_index][0],
                    layer_gathered[layer_branch_index][1],
                    layer_query_ids,
                    layer_key_ids,
                    layer_peak_sets[layer_branch_index],
                    grad_summed,
                    grad_total,
                    scale,
                )
            )
        returned = list([(grad_set[1], grad_set[2]) for grad_set in branch_grads])
        for return_branch_index in range(1, BRANCHES):
            for return_bit_index in reversed(range(branch_items[return_branch_index][1])):
                return_upper = seq_pos // (1 << return_bit_index) % 2 == 1
                keep_part, give_part = split_pair(returned[return_branch_index], return_upper)
                return_received = swapped((give_part[0], give_part[1]), "seq", return_bit_index)
                returned[return_branch_index] = (
                    keep_part[0] + return_received[0],
                    keep_part[1] + return_received[1],
                )
        grad_query_all = jnp.zeros(head_shape, jnp.float32)
        grad_key_all = jnp.zeros(head_shape, jnp.float32)
        grad_value_all = jnp.zeros(head_shape, jnp.float32)
        for layer_branch_index in range(BRANCHES):
            layer_pick_float = branch_items[layer_branch_index][0]
            grad_query_all = grad_query_all + place_rows(
                branch_grads[layer_branch_index][0], layer_pick_float
            )
            grad_key_all = grad_key_all + place_rows(
                returned[layer_branch_index][0], layer_pick_float
            )
            grad_value_all = grad_value_all + place_rows(
                returned[layer_branch_index][1], layer_pick_float
            )
        grad_query_b = grad_query_all.reshape(rows, feat_here).astype(jnp.bfloat16)
        grad_key_b = grad_key_all.reshape(rows, feat_here).astype(jnp.bfloat16)
        grad_value_b = grad_value_all.reshape(rows, feat_here).astype(jnp.bfloat16)
        grad_qkv_b = jnp.stack([grad_query_b, grad_key_b, grad_value_b], axis=1)
        grad_qv_bias = jnp.stack(
            [
                jnp.sum(grad_query_b.astype(jnp.float32), axis=0),
                jnp.sum(grad_value_b.astype(jnp.float32), axis=0),
            ]
        )
        grad_qkv = jnp.einsum(
            "td,tcf->dcf", layer_normed_b, grad_qkv_b, preferred_element_type=jnp.float32
        )
        grad_normed = reduce_heads(grad_qkv_b, w_qkv[layer_index], "tcf,dcf->td")
        norm_pull_one = jax.vjp(norm_rows, layer_current, layer_gains[0], layer_shifts[0])[1]
        grad_input_norm, grad_gain_one, grad_shift_one = norm_pull_one(grad_normed)
        grad_input = grad_resid + grad_input_norm
        local_terms = (
            jnp.stack([grad_gain_one, grad_gain_two]),
            jnp.stack([grad_shift_one, grad_shift_two]),
            grad_qkv,
            grad_qv_bias,
            grad_out_weight,
            grad_out_bias,
            grad_up,
            grad_up_bias,
            grad_down,
            grad_down_bias,
        )
        grad_running, local_terms = (grad_input, local_terms)
        layer_terms[layer_index] = local_terms
    stacked = [
        jnp.stack([layer_set[slot_index] for layer_set in layer_terms]) for slot_index in range(10)
    ]
    (
        grad_gain,
        grad_shift,
        grad_qkv_all,
        grad_qv_all,
        grad_outw_all,
        grad_outb_all,
        grad_up_all,
        grad_upb_all,
        grad_down_all,
        grad_downb_all,
    ) = stacked
    summed_grads = lax.psum(
        (
            grad_gain,
            grad_shift,
            grad_qkv_all,
            grad_qv_all,
            grad_outw_all,
            grad_outb_all,
            grad_up_all,
            grad_upb_all,
            grad_down_all,
            grad_downb_all,
        ),
        "seq",
    )
    return (current.astype(jnp.bfloat16), grad_running) + tuple(summed_grads)


def solution(mesh):
    in_specs = (
        P("seq", None),
        P(),
        P(),
        P(),
        P(None, None, None, "heads"),
        P(None, None, "heads"),
        P(None, "heads", None),
        P(),
        P(None, None, "heads"),
        P(None, "heads"),
        P(None, "heads", None),
        P(),
        P("seq", None),
    )
    out_specs = (
        P("seq", None),
        P("seq", None),
        P(),
        P(),
        P(None, None, None, "heads"),
        P(None, None, "heads"),
        P(None, "heads", None),
        P(),
        P(None, None, "heads"),
        P(None, "heads"),
        P(None, "heads", None),
        P(),
    )
    return jax.shard_map(shards, mesh=mesh, in_specs=in_specs, out_specs=out_specs, check_vma=False)
```

profile of v0, /device:TPU:0, one launch (start us, length us, event | category | flops | bytes accessed | tf_op | source)
XLA Modules:
  0.0 1172.8 jit_solution(8696346169329916000)
XLA Ops:
  18.3 3.3 squeeze.47
  27.5 3.2 squeeze.52
  30.8 5.8 multiply_reduce_fusion.10
  37.8 3.2 squeeze.46
  42.5 3.2 squeeze.51
  46.4 6.0 multiply_reduce_fusion.12
  53.7 3.4 squeeze.45
  58.6 3.2 squeeze.50
  63.1 6.4 multiply_reduce_fusion.14
  72.2 3.2 squeeze.49
  75.4 3.6 squeeze.44
  79.6 7.1 multiply_reduce_fusion.15
  126.6 4.8 fusion
  131.4 5.3 fusion.209
  196.8 3.1 copy.225
  200.0 3.1 fusion.1
  207.5 5.5 convolution_bitcast_fusion.8
  219.2 3.3 mul.850
  222.5 3.1 copy.216
  239.4 3.1 copy.219
  247.8 3.1 convolution_bitcast_fusion.10
  259.2 10.9 fusion.217
  273.4 122.8 %all-reduce.8.cloned.1.call-done = f32[1024,768]{1,0:T(8,128)} async-done(((f32[1024,768]{1,0:T(8,128)}), f32[1024,768]{1,0:T(8,128)}) %all-reduce.8.cloned.1.call-update) | async-done | bytes 3145744 | tf_op jit(solution)/shard_map/psum | solution.py:182
  399.4 9.7 multiply_convert_fusion.3
  417.4 4.9 fusion.93
  422.3 114.0 %all-reduce.10.cloned.1.call-done = f32[1024,768]{1,0:T(8,128)} async-done(((f32[1024,768]{1,0:T(8,128)}), f32[1024,768]{1,0:T(8,128)}) %all-reduce.10.cloned.1.call-update) | async-done | bytes 3145744 | tf_op jit(solution)/shard_map/psum | solution.py:182
  536.3 3.6 multiply_reduce_fusion
  546.0 3.1 copy.241
  556.0 3.1 copy.385
  568.2 3.1 copy.235
  571.2 3.9 multiply_reduce_fusion.3
  576.8 3.3 convolution_bitcast_fusion.4
  583.3 3.1 copy.230
  586.3 5.5 multiply_reduce_fusion.4
  593.7 4.9 convolution_bitcast_fusion.5
  619.2 4.2 multiply_convert_fusion.2
  631.7 7.0 multiply_convert_fusion.1
  645.9 3.1 copy.243
  658.9 3.4 fusion.101
  666.9 3.1 copy.237
  669.9 4.7 fusion.90
  676.9 3.3 mul.922
  683.3 12.4 %multiply_convert_fusion = bf16[4,1024,1024]{1,2,0:T(8,128)(2,1)S(1)} fusion(f32[4,1024]{1,0:T(4,128)} %get-tuple-element.59, f32[1024,4,48]{0,2,1:T(8,128)} %bitcast.454, f32[4,48]{1,0:T(4,128)} %copy-done.122, f32[1024,4,48]{0,2,1:T(8,128)} %copy-done.40, f32[1024,4]{0,1:T(4,128)} %get-tuple-element.60, f32[4,1024]{1,0:T(4,128)} %copy-done.121, ...), kind=kOutput, calls=%fused_computation.3 | convolution fusion | flops 432799744 | bytes 26792704 | tf_op jit(solution)/shard_map/qhe,khe->hqk/dot_general | solution.py:132
  695.7 3.3 copy-done.10
  699.0 3.3 convert_reduce_fusion.4
  706.3 3.1 collective-permute-done.34
  710.1 3.9 collective-permute-done.25
  723.3 3.1 copy.252
  737.0 3.3 mul.980
  740.3 3.1 copy.255
  753.9 3.3 mul.962
  757.2 3.1 copy.246
  768.8 3.1 copy.257
  794.5 3.1 copy.250
  797.7 11.5 convert_reduce_fusion.3
  809.2 6.3 fusion.83
  816.3 3.1 convolution_bitcast_fusion
  819.6 5.0 convolution_bitcast_fusion.1
  824.6 3.3 convolution_bitcast_fusion.2
  833.3 208.6 %all-reduce.14.cloned.1.call-done = (f32[1024,768]{1,0:T(8,128)}, f32[1024,768]{1,0:T(8,128)}) async-done(((f32[1024,768]{1,0:T(8,128)}, f32[1024,768]{1,0:T(8,128)}), (f32[1024,768]{1,0:T(8,128)}, f32[1024,768]{1,0:T(8,128)})) %all-reduce.14.cloned.1.call-update) | async-done | bytes 6291472 | tf_op jit(solution)/shard_map/psum | solution.py:182
  1041.9 3.4 fusion.210
  1050.5 26.2 %all-reduce = (f32[1,2,768]{2,1,0:T(2,128)}, f32[1,2,768]{2,1,0:T(2,128)}, f32[1,2,192]{2,1,0:T(2,128)}, f32[1,768]{1,0:T(1,128)}, f32[1,768]{1,0:T(1,128)}, /*index=5*/f32[1,768]{1,0:T(1,128)}) all-reduce(f32[1,2,768]{2,1,0:T(2,128)S(1)} %maximum_bitcast_fusion, ...), channel_id=1, replica_groups=mesh['seq'=8,'heads'=4] {'seq'}, use_global_device_ids=true, to_apply=%region_37.38 | all-reduce | flops 5760 | bytes 46080 | tf_op jit(solution)/shard_map/psum | solution.py:410
  1076.7 3.5 add_convert_fusion.1
  1080.2 79.2 %all-reduce.12.cloned.1.call-done = (f32[1,768,3,192]{1,3,2,0:T(8,128)}, f32[1,192,768]{2,1,0:T(8,128)}, f32[1,768,768]{2,1,0:T(8,128)}, f32[1,768,768]{2,1,0:T(8,128)}) async-done(((f32[1,768,3,192]{1,3,2,0:T(8,128)}, f32[1,192,768]{2,1,0:T(8,128)}, f32[1,768,768]{2,1,0:T(8,128)}, f32[1,768,768]{2,1,0:T(8,128)}), (f32[1,768,3,192]{1,3,2,0:T(8,128)}, f32[1,192,768]{2,1,0:T(8,128)}, ...) | async-done | bytes 7077904 | tf_op jit(solution)/shard_map/psum | solution.py:410
  (669 shorter events, 348.7 us)
Async XLA Ops:
  7.2 392.0 %copy-start = (bf16[1,768,768]{2,1,0:T(8,128)(2,1)S(1)}, bf16[1,768,768]{2,1,0:T(8,128)(2,1)}, u32[]{:S(2)}) copy-start(bf16[1,768,768]{2,1,0:T(8,128)(2,1)} %param.21) | copy-start | bytes 3538948
  7.2 389.0 %all-reduce.8.cloned.1.call-start = ((), (), s32[]{:S(2)}) async-start(), calls=%async_computation | async-start | bytes 6291456 | tf_op jit(solution)/shard_map/psum | solution.py:182
  15.7 110.8 %copy-start.97 = (f32[4,48]{1,0:T(4,128)}, f32[4,48]{1,0:T(4,128)S(1)}, u32[]{:S(2)}) copy-start(f32[4,48]{1,0:T(4,128)S(1)} %add.439) | copy-start | bytes 2308
  17.0 126.8 %copy-start.131 = (f32[16,4]{0,1:T(4,128)}, f32[16,4]{0,1:T(4,128)S(1)}, u32[]{:S(2)}) copy-start(f32[16,4]{0,1:T(4,128)S(1)} %get-tuple-element.103) | copy-start | bytes 772
  30.8 48.8 %copy-start.122 = (f32[4,48]{1,0:T(4,128)}, f32[4,48]{1,0:T(4,128)S(1)}, u32[]{:S(2)}) copy-start(f32[4,48]{1,0:T(4,128)S(1)} %add.461) | copy-start | bytes 2308
  37.4 120.7 %collective-permute-start.6 = (bf16[64,4,48]{0,2,1:T(8,128)(2,1)}, bf16[64,4,48]{0,2,1:T(8,128)(2,1)}, u32[]{:S(2)}, u32[]{:S(2)}) collective-permute-start(bf16[64,4,48]{0,2,1:T(8,128)(2,1)} %bitcast.393), channel_id=1, source_target_pairs={{0,4},{4,0},{8,12},{12,8},{16,20},{20,16},{24,28},{28,24},{1,5},{5... | collective-permute-start | bytes 73736 | tf_op jit(solution)/shard_map/ppermute | solution.py:16
  53.2 107.4 %collective-permute-start.3 = (bf16[128,4,48]{0,2,1:T(8,128)(2,1)}, bf16[128,4,48]{0,2,1:T(8,128)(2,1)}, u32[]{:S(2)}, u32[]{:S(2)}) collective-permute-start(bf16[128,4,48]{0,2,1:T(8,128)(2,1)} %bitcast.394), channel_id=1, source_target_pairs={{0,4},{4,0},{8,12},{12,8},{16,20},{20,16},{24,28},{28,24},{1,5},{5... | collective-permute-start | bytes 147464 | tf_op jit(solution)/shard_map/ppermute | solution.py:16
  70.3 103.2 %collective-permute-start.1 = (bf16[256,4,48]{0,2,1:T(8,128)(2,1)}, bf16[256,4,48]{0,2,1:T(8,128)(2,1)}, u32[]{:S(2)}, u32[]{:S(2)}) collective-permute-start(bf16[256,4,48]{0,2,1:T(8,128)(2,1)} %bitcast.477), channel_id=1, source_target_pairs={{0,4},{4,0},{8,12},{12,8},{16,20},{20,16},{24,28},{28,24},{1,5},{5... | collective-permute-start | bytes 294920 | tf_op jit(solution)/shard_map/ppermute | solution.py:16
  86.8 39.8 %copy-start.25 = (f32[1024,1,192]{0,2,1:T(8,128)S(1)}, f32[1024,1,192]{0,2,1:T(8,128)}, u32[]{:S(2)}) copy-start(f32[1024,1,192]{0,2,1:T(8,128)} %copy-done.24) | copy-start | bytes 2359300
  88.8 111.1 %collective-permute-start = (bf16[512,4,48]{0,2,1:T(8,128)(2,1)}, bf16[512,4,48]{0,2,1:T(8,128)(2,1)}, u32[]{:S(2)}, u32[]{:S(2)}) collective-permute-start(bf16[512,4,48]{0,2,1:T(8,128)(2,1)} %bitcast.472), channel_id=1, source_target_pairs={{0,4},{4,0},{8,12},{12,8},{16,20},{20,16},{24,28},{28,24},{1,5},{5... | collective-permute-start | bytes 589832 | tf_op jit(solution)/shard_map/ppermute | solution.py:16
  90.4 68.7 %collective-permute-start.15 = (bf16[64,4,48]{0,2,1:T(8,128)(2,1)}, bf16[64,4,48]{0,2,1:T(8,128)(2,1)}, u32[]{:S(2)}, u32[]{:S(2)}) collective-permute-start(bf16[64,4,48]{0,2,1:T(8,128)(2,1)} %bitcast.481), channel_id=1, source_target_pairs={{0,4},{4,0},{8,12},{12,8},{16,20},{20,16},{24,28},{28,24},{1,5},{5... | collective-permute-start | bytes 73736 | tf_op jit(solution)/shard_map/ppermute | solution.py:16
  95.0 36.4 %copy-start.85 = (s32[1024]{0:T(1024)}, s32[1024]{0:T(1024)S(1)}, u32[]{:S(2)}) copy-start(s32[1024]{0:T(1024)S(1)} %dynamic_slice.12) | copy-start | bytes 12292
  137.2 18.3 %copy-start.51 = (bf16[4,512,48]{2,0,1:T(4,128)(2,1)S(1)}, bf16[4,512,48]{2,0,1:T(4,128)(2,1)}, u32[]{:S(2)}) copy-start(bf16[4,512,48]{2,0,1:T(4,128)(2,1)} %get-tuple-element.37) | copy-start | bytes 589828
  142.5 17.1 %copy-start.88 = (bf16[4,64,48]{1,2,0:T(8,128)(2,1)S(1)}, bf16[4,64,48]{1,2,0:T(8,128)(2,1)}, u32[]{:S(2)}) copy-start(bf16[4,64,48]{1,2,0:T(8,128)(2,1)} %copy.355) | copy-start | bytes 73732
  143.8 56.2 %copy-start.64 = (bf16[4,512,48]{1,2,0:T(8,128)(2,1)}, bf16[4,512,48]{1,2,0:T(8,128)(2,1)S(1)}, u32[]{:S(2)}) copy-start(bf16[4,512,48]{1,2,0:T(8,128)(2,1)S(1)} %copy.268) | copy-start | bytes 589828
  148.6 34.0 %copy-start.96 = (s32[512,4]{0,1:T(4,128)S(1)}, s32[512,4]{0,1:T(4,128)}, u32[]{:S(2)}) copy-start(s32[512,4]{0,1:T(4,128)} %multiply_reduce_fusion.22) | copy-start | bytes 24580
  148.6 34.0 %copy-start.139 = (s32[64,4]{0,1:T(4,128)S(1)}, s32[64,4]{0,1:T(4,128)}, u32[]{:S(2)}) copy-start(s32[64,4]{0,1:T(4,128)} %multiply_reduce_fusion.25) | copy-start | bytes 3076
  158.0 3.6 collective-permute-start.12
  159.1 16.2 %collective-permute-start.10 = (bf16[256,4,48]{0,2,1:T(8,128)(2,1)}, bf16[256,4,48]{0,2,1:T(8,128)(2,1)S(1)}, u32[]{:S(2)}, u32[]{:S(2)}) collective-permute-start(bf16[256,4,48]{0,2,1:T(8,128)(2,1)} %bitcast.479), channel_id=1, source_target_pairs={{0,4},{4,0},{8,12},{12,8},{16,20},{20,16},{24,28},{28,24},{1,5},{5... | collective-permute-start | bytes 294920 | tf_op jit(solution)/shard_map/ppermute | solution.py:16
  160.6 46.9 %collective-permute-start.9 = (bf16[512,4,48]{0,2,1:T(8,128)(2,1)}, bf16[512,4,48]{0,2,1:T(8,128)(2,1)}, u32[]{:S(2)}, u32[]{:S(2)}) collective-permute-start(bf16[512,4,48]{0,2,1:T(8,128)(2,1)} %bitcast.483), channel_id=1, source_target_pairs={{0,4},{4,0},{8,12},{12,8},{16,20},{20,16},{24,28},{28,24},{1,5},{5... | collective-permute-start | bytes 589832 | tf_op jit(solution)/shard_map/ppermute | solution.py:16
  161.6 5.1 collective-permute-start.7
  166.7 4.1 collective-permute-start.16
  170.8 8.2 collective-permute-start.4
  173.5 6.3 collective-permute-start.13
  175.3 7.3 collective-permute-start.8
  179.0 9.8 collective-permute-start.17
  179.8 45.8 %collective-permute-start.2 = (bf16[512,4,48]{0,2,1:T(8,128)(2,1)}, bf16[512,4,48]{0,2,1:T(8,128)(2,1)}, u32[]{:S(2)}, u32[]{:S(2)}) collective-permute-start(bf16[512,4,48]{0,2,1:T(8,128)(2,1)} %maximum_select_fusion.6), channel_id=1, source_target_pairs={{0,8},{4,12},{8,0},{12,4},{16,24},{20,28},{24,16},{28,20},{1,9},{5... | collective-permute-start | bytes 589832 | tf_op jit(solution)/shard_map/ppermute | solution.py:16
  182.5 47.0 %collective-permute-start.11 = (bf16[512,4,48]{0,2,1:T(8,128)(2,1)}, bf16[512,4,48]{0,2,1:T(8,128)(2,1)}, u32[]{:S(2)}, u32[]{:S(2)}) collective-permute-start(bf16[512,4,48]{0,2,1:T(8,128)(2,1)} %maximum_select_fusion.9), channel_id=1, source_target_pairs={{0,8},{4,12},{8,0},{12,4},{16,24},{20,28},{24,16},{28,20},{1,9},{5... | collective-permute-start | bytes 589832 | tf_op jit(solution)/shard_map/ppermute | solution.py:16
  183.8 16.1 %copy-start.54 = (f32[4,64,512]{2,1,0:T(8,128)}, f32[4,64,512]{2,1,0:T(8,128)S(1)}, u32[]{:S(2)}) copy-start(f32[4,64,512]{2,1,0:T(8,128)S(1)} %get-tuple-element.116) | copy-start | bytes 1572868
  183.8 16.1 %copy-start.138 = (f32[4,64]{1,0:T(4,128)}, f32[4,64]{1,0:T(4,128)S(1)}, u32[]{:S(2)}) copy-start(f32[4,64]{1,0:T(4,128)S(1)} %get-tuple-element.115) | copy-start | bytes 3076
  188.8 53.7 %collective-permute-start.5 = (bf16[512,4,48]{0,2,1:T(8,128)(2,1)}, bf16[512,4,48]{0,2,1:T(8,128)(2,1)}, u32[]{:S(2)}, u32[]{:S(2)}) collective-permute-start(bf16[512,4,48]{0,2,1:T(8,128)(2,1)} %maximum_select_fusion.7), channel_id=1, source_target_pairs={{0,16},{4,20},{8,24},{12,28},{16,0},{20,4},{24,8},{28,12},{1,17},{... | collective-permute-start | bytes 589832 | tf_op jit(solution)/shard_map/ppermute | solution.py:16
  199.9 47.9 %collective-permute-start.14 = (bf16[512,4,48]{0,2,1:T(8,128)(2,1)}, bf16[512,4,48]{0,2,1:T(8,128)(2,1)}, u32[]{:S(2)}, u32[]{:S(2)}) collective-permute-start(bf16[512,4,48]{0,2,1:T(8,128)(2,1)} %maximum_select_fusion.10), channel_id=1, source_target_pairs={{0,16},{4,20},{8,24},{12,28},{16,0},{20,4},{24,8},{28,12},{1,17},{... | collective-permute-start | bytes 589832 | tf_op jit(solution)/shard_map/ppermute | solution.py:16
  273.3 263.1 %all-reduce.10.cloned.1.call-start = ((), (), s32[]{:S(2)}) async-start(), calls=%async_computation.1 | async-start | bytes 6291456 | tf_op jit(solution)/shard_map/psum | solution.py:182
  398.7 141.3 %copy-start.101 = (f32[1024]{0:T(1024)}, f32[1024]{0:T(1024)S(1)}, u32[]{:S(2)}) copy-start(f32[1024]{0:T(1024)S(1)} %broadcast_multiply_fusion.4) | copy-start | bytes 12292
  399.2 140.7 %copy-start.127 = (f32[1024]{0:T(1024)}, f32[1024]{0:T(1024)S(1)}, u32[]{:S(2)}) copy-start(f32[1024]{0:T(1024)S(1)} %fusion.166) | copy-start | bytes 12292
  416.1 625.8 %all-reduce.14.cloned.1.call-start = ((), (), s32[]{:S(2)}) async-start(), calls=%async_computation.3 | async-start | bytes 12582912 | tf_op jit(solution)/shard_map/psum | solution.py:182
  417.4 118.9 %copy-start.3 = (f32[1024,768]{1,0:T(8,128)S(1)}, f32[1024,768]{1,0:T(8,128)}, u32[]{:S(2)}) copy-start(f32[1024,768]{1,0:T(8,128)} %copy-done.2) | copy-start | bytes 9437188
  554.5 148.6 %collective-permute-start.33 = (f32[256,4,48]{0,2,1:T(8,128)}, f32[256,4,48]{0,2,1:T(8,128)}, u32[]{:S(2)}, u32[]{:S(2)}) collective-permute-start(f32[256,4,48]{0,2,1:T(8,128)} %slice_select_fusion.6), channel_id=1, source_target_pairs={{0,16},{4,20},{8,24},{12,28},{16,0},{20,4},{24,8},{28,12},{1,17},{... | collective-permute-start | bytes 589832 | tf_op jit(solution)/shard_map/ppermute | solution.py:16
  567.6 158.7 %collective-permute-start.30 = (f32[512,4,48]{0,2,1:T(8,128)}, f32[512,4,48]{0,2,1:T(8,128)}, u32[]{:S(2)}, u32[]{:S(2)}) collective-permute-start(f32[512,4,48]{0,2,1:T(8,128)} %slice_select_fusion), channel_id=1, source_target_pairs={{0,16},{4,20},{8,24},{12,28},{16,0},{20,4},{24,8},{28,12},{1,17},{... | collective-permute-start | bytes 1179656 | tf_op jit(solution)/shard_map/ppermute | solution.py:16
  581.8 146.7 %collective-permute-start.28 = (f32[512,4,48]{0,2,1:T(8,128)}, f32[512,4,48]{0,2,1:T(8,128)}, u32[]{:S(2)}, u32[]{:S(2)}) collective-permute-start(f32[512,4,48]{0,2,1:T(8,128)} %slice_select_fusion.1), channel_id=1, source_target_pairs={{0,8},{4,12},{8,0},{12,4},{16,24},{20,28},{24,16},{28,20},{1,9},{5... | collective-permute-start | bytes 1179656 | tf_op jit(solution)/shard_map/ppermute | solution.py:16
  600.2 132.6 %collective-permute-start.27 = (f32[512,4,48]{0,2,1:T(8,128)}, f32[512,4,48]{0,2,1:T(8,128)}, u32[]{:S(2)}, u32[]{:S(2)}) collective-permute-start(f32[512,4,48]{0,2,1:T(8,128)} %slice_select_fusion.2), channel_id=1, source_target_pairs={{0,4},{4,0},{8,12},{12,8},{16,20},{20,16},{24,28},{28,24},{1,5},{5... | collective-permute-start | bytes 1179656 | tf_op jit(solution)/shard_map/ppermute | solution.py:16
  606.8 97.9 %collective-permute-start.24 = (f32[256,4,48]{0,2,1:T(8,128)}, f32[256,4,48]{0,2,1:T(8,128)}, u32[]{:S(2)}, u32[]{:S(2)}) collective-permute-start(f32[256,4,48]{0,2,1:T(8,128)} %slice_select_fusion.9), channel_id=1, source_target_pairs={{0,16},{4,20},{8,24},{12,28},{16,0},{20,4},{24,8},{28,12},{1,17},{... | collective-permute-start | bytes 589832 | tf_op jit(solution)/shard_map/ppermute | solution.py:16
  683.2 15.7 %copy-start.34 = (bf16[1024,1,192]{0,2,1:T(8,128)(2,1)S(1)}, bf16[1024,1,192]{0,2,1:T(8,128)(2,1)}, u32[]{:S(2)}) copy-start(bf16[1024,1,192]{0,2,1:T(8,128)(2,1)} %slice.340) | copy-start | bytes 1179652
  683.3 15.7 %copy-start.44 = (f32[1024,4,48]{0,2,1:T(8,128)S(1)}, f32[1024,4,48]{0,2,1:T(8,128)}, u32[]{:S(2)}) copy-start(f32[1024,4,48]{0,2,1:T(8,128)} %copy.243) | copy-start | bytes 2359300
  683.3 15.7 %copy-start.45 = (f32[1024,4,48]{0,2,1:T(8,128)S(1)}, f32[1024,4,48]{0,2,1:T(8,128)}, u32[]{:S(2)}) copy-start(f32[1024,4,48]{0,2,1:T(8,128)} %copy.240) | copy-start | bytes 2359300
  683.3 15.7 %copy-start.47 = (f32[1024,4,48]{0,2,1:T(8,128)S(1)}, f32[1024,4,48]{0,2,1:T(8,128)}, u32[]{:S(2)}) copy-start(f32[1024,4,48]{0,2,1:T(8,128)} %copy.237) | copy-start | bytes 2359300
  683.3 15.7 %copy-start.48 = (f32[1024,4,48]{0,2,1:T(8,128)S(1)}, f32[1024,4,48]{0,2,1:T(8,128)}, u32[]{:S(2)}) copy-start(f32[1024,4,48]{0,2,1:T(8,128)} %copy.234) | copy-start | bytes 2359300
  683.3 15.7 %copy-start.72 = (f32[1024,4]{0,1:T(4,128)S(1)}, f32[1024,4]{0,1:T(4,128)}, u32[]{:S(2)}) copy-start(f32[1024,4]{0,1:T(4,128)} %mul.869) | copy-start | bytes 49156
  683.3 15.7 %copy-start.74 = (f32[1024,4]{0,1:T(4,128)S(1)}, f32[1024,4]{0,1:T(4,128)}, u32[]{:S(2)}) copy-start(f32[1024,4]{0,1:T(4,128)} %mul.861) | copy-start | bytes 49156
  703.1 40.3 %collective-permute-start.21 = (f32[512,4,48]{0,2,1:T(8,128)}, f32[512,4,48]{0,2,1:T(8,128)}, u32[]{:S(2)}, u32[]{:S(2)}) collective-permute-start(f32[512,4,48]{0,2,1:T(8,128)} %slice_select_fusion.3), channel_id=1, source_target_pairs={{0,16},{4,20},{8,24},{12,28},{16,0},{20,4},{24,8},{28,12},{1,17},{... | collective-permute-start | bytes 1179656 | tf_op jit(solution)/shard_map/ppermute | solution.py:16
  704.7 4.7 collective-permute-start.34
  709.4 4.6 collective-permute-start.25
  714.0 1.3 collective-permute-start.35
  715.3 4.9 collective-permute-start.26
  720.2 26.6 %collective-permute-start.19 = (f32[512,4,48]{0,2,1:T(8,128)}, f32[512,4,48]{0,2,1:T(8,128)}, u32[]{:S(2)}, u32[]{:S(2)}) collective-permute-start(f32[512,4,48]{0,2,1:T(8,128)} %slice_select_fusion.4), channel_id=1, source_target_pairs={{0,8},{4,12},{8,0},{12,4},{16,24},{20,28},{24,16},{28,20},{1,9},{5... | collective-permute-start | bytes 1179656 | tf_op jit(solution)/shard_map/ppermute | solution.py:16
  726.4 23.4 %collective-permute-start.18 = (f32[512,4,48]{0,2,1:T(8,128)}, f32[512,4,48]{0,2,1:T(8,128)}, u32[]{:S(2)}, u32[]{:S(2)}) collective-permute-start(f32[512,4,48]{0,2,1:T(8,128)} %slice_select_fusion.5), channel_id=1, source_target_pairs={{0,4},{4,0},{8,12},{12,8},{16,20},{20,16},{24,28},{28,24},{1,5},{5... | collective-permute-start | bytes 1179656 | tf_op jit(solution)/shard_map/ppermute | solution.py:16
  728.5 31.7 %collective-permute-start.31 = (f32[256,4,48]{0,2,1:T(8,128)}, f32[256,4,48]{0,2,1:T(8,128)}, u32[]{:S(2)}, u32[]{:S(2)}) collective-permute-start(f32[256,4,48]{0,2,1:T(8,128)} %slice_select_fusion.7), channel_id=1, source_target_pairs={{0,8},{4,12},{8,0},{12,4},{16,24},{20,28},{24,16},{28,20},{1,9},{5... | collective-permute-start | bytes 589832 | tf_op jit(solution)/shard_map/ppermute | solution.py:16
  732.8 29.5 %collective-permute-start.29 = (f32[256,4,48]{0,2,1:T(8,128)}, f32[256,4,48]{0,2,1:T(8,128)}, u32[]{:S(2)}, u32[]{:S(2)}) collective-permute-start(f32[256,4,48]{0,2,1:T(8,128)} %slice_select_fusion.8), channel_id=1, source_target_pairs={{0,4},{4,0},{8,12},{12,8},{16,20},{20,16},{24,28},{28,24},{1,5},{5... | collective-permute-start | bytes 589832 | tf_op jit(solution)/shard_map/ppermute | solution.py:16
  746.2 25.7 %collective-permute-start.22 = (f32[256,4,48]{0,2,1:T(8,128)}, f32[256,4,48]{0,2,1:T(8,128)}, u32[]{:S(2)}, u32[]{:S(2)}) collective-permute-start(f32[256,4,48]{0,2,1:T(8,128)} %slice_select_fusion.10), channel_id=1, source_target_pairs={{0,8},{4,12},{8,0},{12,4},{16,24},{20,28},{24,16},{28,20},{1,9},{5... | collective-permute-start | bytes 589832 | tf_op jit(solution)/shard_map/ppermute | solution.py:16
  749.6 24.2 %collective-permute-start.20 = (f32[256,4,48]{0,2,1:T(8,128)}, f32[256,4,48]{0,2,1:T(8,128)}, u32[]{:S(2)}, u32[]{:S(2)}) collective-permute-start(f32[256,4,48]{0,2,1:T(8,128)} %slice_select_fusion.11), channel_id=1, source_target_pairs={{0,4},{4,0},{8,12},{12,8},{16,20},{20,16},{24,28},{28,24},{1,5},{5... | collective-permute-start | bytes 589832 | tf_op jit(solution)/shard_map/ppermute | solution.py:16
  762.0 19.7 %collective-permute-start.32 = (f32[128,4,48]{0,2,1:T(8,128)}, f32[128,4,48]{0,2,1:T(8,128)}, u32[]{:S(2)}, u32[]{:S(2)}) collective-permute-start(f32[128,4,48]{0,2,1:T(8,128)} %slice_select_fusion.14), channel_id=1, source_target_pairs={{0,4},{4,0},{8,12},{12,8},{16,20},{20,16},{24,28},{28,24},{1,5},{5... | collective-permute-start | bytes 294920 | tf_op jit(solution)/shard_map/ppermute | solution.py:16
  773.6 16.9 %collective-permute-start.23 = (f32[128,4,48]{0,2,1:T(8,128)}, f32[128,4,48]{0,2,1:T(8,128)}, u32[]{:S(2)}, u32[]{:S(2)}) collective-permute-start(f32[128,4,48]{0,2,1:T(8,128)} %slice_select_fusion.17), channel_id=1, source_target_pairs={{0,4},{4,0},{8,12},{12,8},{16,20},{20,16},{24,28},{28,24},{1,5},{5... | collective-permute-start | bytes 294920 | tf_op jit(solution)/shard_map/ppermute | solution.py:16
  819.5 339.9 %all-reduce.12.cloned.1.call-start = ((), (), s32[]{:S(2)}) async-start(), calls=%async_computation.2 | async-start | bytes 14155776 | tf_op jit(solution)/shard_map/psum | solution.py:410
  833.0 212.3 %copy-start.130 = (f32[1024]{0:T(1024)S(1)}, f32[1024]{0:T(1024)}, u32[]{:S(2)}) copy-start(f32[1024]{0:T(1024)} %copy-done.129) | copy-start | bytes 12292
  (150 other events, 692.0 us)
Sparse Core Ops, SparseCore 0:
  273.4 122.7 all-reduce.7
  416.2 120.0 all-reduce.9
  819.6 222.2 all-reduce.13
  1046.5 112.8 all-reduce.11
where the time goes:
time: 1180 us; the launch traced here: 1170 us
  waiting for transfers between devices  536 us (45%)
  local copies, waits for them, and re-layouts  272 us (23%)
  matrix products  157 us (13%)
  other arithmetic  140 us (12%)
  blocking collectives  26.2 us (2%)
  starting transfers between devices  25.9 us (2%)
  between operations  16.2 us (1%)
    psum x3, waiting for transfers between devices, reduce_heads(): lax.psum(jnp.einsum(form, left, weight, preferred_element_type=jnp.float3...  445 us
    mul x40, local copies, waits for them, and re-layouts, place_rows(): values[:, None] * pick_float[None, :, :, None]  98.1 us
    psum x1, waiting for transfers between devices, shards(): lax.psum((grad_gain, grad_shift, grad_qkv_all, grad_qv_all, grad_outw_all...  79.2 us
    unnamed x13, other arithmetic  39.6 us
    unnamed x357, local copies, waits for them, and re-layouts  31.5 us
    dot_general x5, matrix products, attend_backward(): jnp.einsum('qhe,khe->hqk', grad_summed, value_rows, preferred_element_typ...  28 us
    psum x1, blocking collectives, shards(): lax.psum((grad_gain, grad_shift, grad_qkv_all, grad_qv_all, grad_outw_all...  26.2 us
    ppermute x36, starting transfers between devices, swapped(): lax.ppermute(array, axis, [(i, i ^ 1 << bit) for i in range(lax.axis_size...  25.8 us
  transfers between devices with their start and end apart: 40, of which 9 were waited for; matrix products, arithmetic and copies ran while one was open for 36% of the time, Pallas kernels for 0%

commit v1 on v0

v1 whole, which is shorter than its diff:
```python
import functools
import math

import jax
import jax.numpy as jnp
import ml_dtypes
import numpy as np
from jax import lax
from jax.experimental import pallas as pl
from jax.experimental.pallas import tpu as pltpu
from jax.sharding import PartitionSpec as P

HEAD_DIM = 48
BRANCHES = 5
DOCS = 3
TOP = BRANCHES - 1
STRIDE = 2**TOP
LANES = 128
EPSILON = 1e-05
BIG = 2.0**100
SCALE = HEAD_DIM**-0.5
LOG2E = math.log2(math.e)
LN2 = math.log(2.0)
DOC_LANE = HEAD_DIM
MULT_LANE = DOC_LANE + DOCS
LSE_LANE = MULT_LANE + 2 * TOP
VALUE_LANE = LANES // 2
ONE_LANE = VALUE_LANE + HEAD_DIM
F32 = jnp.float32
BF16 = jnp.bfloat16
VMEM_LIMIT = 48 * 1024 * 1024


def bit_reversed(block):
    return sum(((block >> bit) & 1) << (TOP - 1 - bit) for bit in range(TOP))


def level_columns(rows):
    table = np.zeros((rows, LANES), np.float32)
    for level in range(1, TOP + 1):
        table[: rows >> level, MULT_LANE + level - 1] = 1.0
        table[: rows >> level, MULT_LANE + TOP + level - 1] = 1.0
    return table.astype(ml_dtypes.bfloat16)


def count_columns(rows, groups):
    table = np.zeros((groups, rows, LANES), np.float32)
    for group in range(groups):
        for level in range(group + 1, TOP + 1):
            step = math.log2((level - group + 1) / (level - group))
            high = float(np.float32(step).astype(ml_dtypes.bfloat16))
            table[group, : rows >> level, MULT_LANE + level - 1] = high
            table[group, : rows >> level, MULT_LANE + TOP + level - 1] = step - high
    return table.astype(ml_dtypes.bfloat16)


def spread_table(heads, first_lane):
    table = np.zeros((heads * HEAD_DIM, heads * LANES), np.float32)
    for head in range(heads):
        for item in range(HEAD_DIM):
            table[head * HEAD_DIM + item, head * LANES + first_lane + item] = 1.0
    return table.astype(ml_dtypes.bfloat16)


def dot_nn(left, right):
    return jnp.dot(left, right, preferred_element_type=F32)


def dot_nt(left, right):
    return lax.dot_general(left, right, (((1,), (1,)), ((), ())), preferred_element_type=F32)


def dot_tn(left, right):
    return lax.dot_general(left, right, (((0,), (0,)), ((), ())), preferred_element_type=F32)


def norm_rows(values, gain_row, shift_row):
    center = values - jnp.mean(values, axis=-1, keepdims=True)
    spread = jnp.mean(center * center, axis=-1, keepdims=True)
    return center * lax.rsqrt(spread + EPSILON) * gain_row + shift_row


def norm_back(values, gain_row, grad_rows):
    center = values - jnp.mean(values, axis=-1, keepdims=True)
    spread = jnp.mean(center * center, axis=-1, keepdims=True)
    inverse = lax.rsqrt(spread + EPSILON)
    unit = center * inverse
    scaled = grad_rows * gain_row
    grad_in = inverse * (
        scaled
        - jnp.mean(scaled, axis=-1, keepdims=True)
        - unit * jnp.mean(scaled * unit, axis=-1, keepdims=True)
    )
    return grad_in, jnp.sum(grad_rows * unit, axis=0), jnp.sum(grad_rows, axis=0)


def full_spec(shape):
    return pl.BlockSpec(shape, lambda *_: (0,) * len(shape))


def head_spec(rows):
    return pl.BlockSpec((1, rows, LANES), lambda head, *_: (head, 0, 0))


SMALL_SPEC = pl.BlockSpec(memory_space=pltpu.SMEM)


def project_kernel(
    first_ref, x_ref, gain_ref, shift_ref, w_ref, bias_ref, fq_ref, fkv_ref, level_ref, spread_k_ref, spread_v_ref,
    normed_ref, q_ref, kv_ref, q_rows, kv_rows,
):
    step = pl.program_id(0)
    tile = x_ref.shape[0]
    heads, rows = q_ref.shape[0], q_ref.shape[1]
    block = rows // STRIDE
    normed = norm_rows(x_ref[...].astype(F32), gain_ref[...], shift_ref[...]).astype(BF16)
    normed_ref[...] = normed
    query = ((dot_nn(normed, w_ref[0]) + bias_ref[0:1]) * (SCALE * LOG2E)).astype(BF16)
    key = dot_nn(normed, w_ref[1]).astype(BF16)
    value = (dot_nn(normed, w_ref[2]) + bias_ref[1:2]).astype(BF16)
    query_wide = dot_nn(query, spread_k_ref[...])
    pair_wide = dot_nn(key, spread_k_ref[...]) + dot_nn(value, spread_v_ref[...])
    here = pl.ds(pl.multiple_of(step * tile, tile), tile)
    for head in range(heads):
        lanes = slice(head * LANES, (head + 1) * LANES)
        q_rows[head, here, :] = query_wide[:, lanes] + fq_ref[...]
        kv_rows[head, here, :] = pair_wide[:, lanes] + fkv_ref[...]

    @pl.when(step == pl.num_programs(0) - 1)
    def _():
        for head in range(heads):
            turn = (first_ref[0] + head) & (STRIDE - 1)
            for item in range(STRIDE):
                start = bit_reversed(item) ^ turn
                there = slice(item * block, (item + 1) * block)
                q_ref[head, there, :] = q_rows[head, pl.ds(start, block, stride=STRIDE), :].astype(BF16)
                kv_ref[head, there, :] = (
                    kv_rows[head, pl.ds(start, block, stride=STRIDE), :] + level_ref[there, :].astype(F32)
                ).astype(BF16)


def project(first, tokens, gain, shift, weights, bias, fq, fkv):
    rows, width = tokens.shape
    feats = weights.shape[2]
    heads = feats // HEAD_DIM
    tile = min(rows, 256)
    row_spec = pl.BlockSpec((tile, width), lambda i: (i, 0))
    lane_spec = pl.BlockSpec((tile, LANES), lambda i: (i, 0))
    shape = (heads, rows, LANES)
    return pl.pallas_call(
        project_kernel,
        grid=(rows // tile,),
        in_specs=[
            SMALL_SPEC, row_spec, full_spec((1, width)), full_spec((1, width)), full_spec(weights.shape),
            full_spec(bias.shape), lane_spec, lane_spec, full_spec((rows, LANES)),
            full_spec((feats, heads * LANES)), full_spec((feats, heads * LANES)),
        ],
        out_specs=[row_spec, full_spec(shape), full_spec(shape)],
        out_shape=[
            jax.ShapeDtypeStruct((rows, width), BF16),
            jax.ShapeDtypeStruct(shape, BF16),
            jax.ShapeDtypeStruct(shape, BF16),
        ],
        scratch_shapes=[pltpu.VMEM(shape, F32), pltpu.VMEM(shape, F32)],
        compiler_params=pltpu.CompilerParams(vmem_limit_bytes=VMEM_LIMIT),
        name="project",
    )(
        first, tokens, gain, shift, weights, bias, fq, fkv, level_columns(rows),
        spread_table(heads, 0), spread_table(heads, VALUE_LANE),
    )


def group_of(distance):
    return distance.bit_length()


def row_tiles(rows, smallest):
    edges = [0, smallest] if smallest < 128 else [0]
    while edges[-1] < rows:
        edges.append(min(rows, edges[-1] - edges[-1] % 128 + 128))
    return list(zip(edges[:-1], edges[1:]))


def attend_kernel(distances, first_ref, q_ref, kv_ref, count_ref, gather_ref, *refs):
    far_refs = refs[: len(distances)]
    out_ref, joined_ref, placed = refs[len(distances) :]
    head = pl.program_id(0)
    rows = q_ref.shape[1]
    block = rows // STRIDE
    turn = (first_ref[0] + head) & (STRIDE - 1)
    smallest = min([rows] + [ref.shape[1] for ref in far_refs])
    for low, high in row_tiles(rows, smallest):
        query = q_ref[0, low:high, :]
        pieces = [(kv_ref, 0)] + [
            (ref, group_of(distance)) for distance, ref in zip(distances, far_refs) if low < ref.shape[1]
        ]
        scores = [dot_nt(query + count_ref[group, low:high, :], ref[0]) for ref, group in pieces]
        peak = functools.reduce(jnp.maximum, [jnp.max(item, axis=-1, keepdims=True) for item in scores])
        total = functools.reduce(
            jnp.add,
            [dot_nn(jnp.exp2(item - peak).astype(BF16), ref[0]) for item, (ref, _) in zip(scores, pieces)],
        )
        mass = total[:, ONE_LANE : ONE_LANE + 1]
        result = total * (1.0 / mass)
        lane = lax.broadcasted_iota(jnp.int32, result.shape, 1)
        out_ref[0, low:high, :] = jnp.where(lane == 0, peak + jnp.log2(mass), result)
        for offset in range(low, high, block):
            start = bit_reversed(offset // block) ^ turn
            placed[head, pl.ds(start, block, stride=STRIDE), :] = result[offset - low : offset - low + block]

    @pl.when(head == pl.num_programs(0) - 1)
    def _():
        joined_ref[...] = functools.reduce(
            jnp.add,
            [
                dot_nn(placed[item].astype(BF16), gather_ref[item * LANES : (item + 1) * LANES])
                for item in range(placed.shape[0])
            ],
        ).astype(BF16)


def attend(first, queries, pairs, far, distances, counts):
    heads, rows, _ = queries.shape
    feats = heads * HEAD_DIM
    gather = spread_table(heads, VALUE_LANE).T.copy()
    return pl.pallas_call(
        functools.partial(attend_kernel, distances),
        grid=(heads,),
        in_specs=[SMALL_SPEC, head_spec(rows), head_spec(rows), full_spec(counts.shape), full_spec(gather.shape)]
        + [head_spec(item.shape[1]) for item in far],
        out_specs=[head_spec(rows), full_spec((rows, feats))],
        out_shape=[
            jax.ShapeDtypeStruct((heads, rows, LANES), F32),
            jax.ShapeDtypeStruct((rows, feats), BF16),
        ],
        scratch_shapes=[pltpu.VMEM((heads, rows, LANES), F32)],
        compiler_params=pltpu.CompilerParams(vmem_limit_bytes=VMEM_LIMIT),
        name="attend",
    )(first, queries, pairs, counts, gather, *far)


def three_parts(values):
    high = values.astype(BF16).astype(F32)
    middle = (values - high).astype(BF16).astype(F32)
    return high, middle, values - high - middle


def attend_back_kernel(distances, first_ref, grad_ref, spread_ref, q_ref, kv_ref, out_ref, count_ref, *refs):
    far_refs = refs[: len(distances)]
    dq_ref, dkv_ref = refs[len(distances) : len(distances) + 2]
    dfar_refs = refs[len(distances) + 2 : 2 * len(distances) + 2]
    wide, query, grad = refs[2 * len(distances) + 2 :]
    head = pl.program_id(0)
    rows = q_ref.shape[1]
    block = rows // STRIDE
    turn = (first_ref[0] + head) & (STRIDE - 1)

    @pl.when(head == 0)
    def _():
        for item in range(wide.shape[0]):
            wide[item] = dot_nn(grad_ref[...], spread_ref[:, item * LANES : (item + 1) * LANES])

    for item in range(STRIDE):
        there = slice(item * block, (item + 1) * block)
        start = bit_reversed(item) ^ turn
        rows_grad = wide[head, pl.ds(start, block, stride=STRIDE), :]
        rows_out = out_ref[0, there, :]
        lane = lax.broadcasted_iota(jnp.int32, rows_grad.shape, 1)
        rows_query = q_ref[0, there, :].astype(F32)
        parts = three_parts(jnp.sum(rows_grad * rows_out, axis=-1, keepdims=True))
        for index, part in enumerate(parts):
            rows_grad = jnp.where(lane == ONE_LANE + index, -part, rows_grad)
        for index, part in enumerate(three_parts(rows_out[:, 0:1])):
            rows_query = jnp.where(lane == LSE_LANE + index, -part, rows_query)
        grad[there, :] = rows_grad.astype(BF16)
        query[there, :] = rows_query.astype(BF16)

    def one(keys, last, group, dq_first):
        counted = query[:last, :] + count_ref[group, :last, :]
        prob = jnp.exp2(dot_nt(keys, counted))
        slope = (prob * dot_nt(keys, grad[:last, :])).astype(BF16)
        dkv = dot_nn(prob.astype(BF16), grad[:last, :]) + dot_nn(slope, query[:last, :])
        dq = dot_tn(slope, keys)
        if dq_first:
            dq_ref[0, :last, :] = dq
        else:
            dq_ref[0, :last, :] += dq
        return dkv

    tile = min(rows, 256)
    for low in range(0, rows, tile):
        dkv_ref[0, low : low + tile, :] = one(kv_ref[0, low : low + tile, :], rows, 0, low == 0)
    for distance, ref, dref in zip(distances, far_refs, dfar_refs):
        count = ref.shape[1]
        step = min(count, tile)
        for low in range(0, count, step):
            dref[0, low : low + step, :] = one(
                ref[0, low : low + step, :], count, group_of(distance), False
            ).astype(BF16)


def attend_back(first, grads, queries, pairs, outs, far, distances, counts):
    heads, rows, _ = queries.shape
    feats = heads * HEAD_DIM
    spread = spread_table(heads, VALUE_LANE)
    return pl.pallas_call(
        functools.partial(attend_back_kernel, distances),
        grid=(heads,),
        in_specs=[
            SMALL_SPEC, full_spec((rows, feats)), full_spec(spread.shape), head_spec(rows), head_spec(rows),
            head_spec(rows), full_spec(counts.shape),
        ]
        + [head_spec(item.shape[1]) for item in far],
        out_specs=[head_spec(rows), head_spec(rows)] + [head_spec(item.shape[1]) for item in far],
        out_shape=[
            jax.ShapeDtypeStruct((heads, rows, LANES), F32),
            jax.ShapeDtypeStruct((heads, rows, LANES), F32),
        ]
        + [jax.ShapeDtypeStruct(item.shape, BF16) for item in far],
        scratch_shapes=[
            pltpu.VMEM((heads, rows, LANES), F32),
            pltpu.VMEM((rows, LANES), BF16),
            pltpu.VMEM((rows, LANES), BF16),
        ],
        compiler_params=pltpu.CompilerParams(vmem_limit_bytes=VMEM_LIMIT),
        name="attend_back",
    )(first, grads, spread, queries, pairs, outs, counts, *far)


def collect_kernel(count, first_ref, dq_ref, dkv_ref, gather_k_ref, gather_v_ref, *refs):
    far_refs = refs[:count]
    outs = refs[count : count + 3]
    q_rows, kv_rows = refs[count + 3 :]
    head = pl.program_id(0)
    rows = dq_ref.shape[1]
    block = rows // STRIDE
    turn = (first_ref[0] + head) & (STRIDE - 1)
    for item in range(STRIDE):
        there = slice(item * block, (item + 1) * block)
        start = bit_reversed(item) ^ turn
        pair = dkv_ref[0, there, :]
        for ref in far_refs:
            if item * block < ref.shape[1]:
                pair = pair + ref[0, there, :].astype(F32)
        lane = lax.broadcasted_iota(jnp.int32, pair.shape, 1)
        q_rows[head, pl.ds(start, block, stride=STRIDE), :] = dq_ref[0, there, :] * SCALE
        kv_rows[head, pl.ds(start, block, stride=STRIDE), :] = jnp.where(lane < VALUE_LANE, pair * LN2, pair)

    @pl.when(head == pl.num_programs(0) - 1)
    def _():
        total = [None] * 3
        for item in range(q_rows.shape[0]):
            lanes = slice(item * LANES, (item + 1) * LANES)
            query = q_rows[item].astype(BF16)
            pair = kv_rows[item].astype(BF16)
            terms = (
                dot_nn(query, gather_k_ref[lanes]),
                dot_nn(pair, gather_k_ref[lanes]),
                dot_nn(pair, gather_v_ref[lanes]),
            )
            total = [term if old is None else old + term for old, term in zip(total, terms)]
        for ref, value in zip(outs, total):
            ref[...] = value.astype(BF16)


def collect(first, dq, dkv, far):
    heads, rows, _ = dq.shape
    feats = heads * HEAD_DIM
    gather_k = spread_table(heads, 0).T.copy()
    gather_v = spread_table(heads, VALUE_LANE).T.copy()
    return pl.pallas_call(
        functools.partial(collect_kernel, len(far)),
        grid=(heads,),
        in_specs=[SMALL_SPEC, head_spec(rows), head_spec(rows), full_spec(gather_k.shape), full_spec(gather_v.shape)]
        + [head_spec(item.shape[1]) for item in far],
        out_specs=[full_spec((rows, feats))] * 3,
        out_shape=[jax.ShapeDtypeStruct((rows, feats), BF16)] * 3,
        scratch_shapes=[pltpu.VMEM((heads, rows, LANES), F32), pltpu.VMEM((heads, rows, LANES), F32)],
        compiler_params=pltpu.CompilerParams(vmem_limit_bytes=VMEM_LIMIT),
        name="collect",
    )(first, dq, dkv, gather_k, gather_v, *far)


def flipped(array, distance):
    return lax.ppermute(array, "seq", [(i, i ^ distance) for i in range(lax.axis_size("seq"))])


def shards(tokens, docs, ln_gain, ln_bias, w_qkv, b_qv, w_out, b_out, w_up, b_up, w_down, b_down, cotangent):
    rows, width = tokens.shape
    feats = w_qkv.shape[3]
    heads = feats // HEAD_DIM
    seq_count = lax.axis_size("seq")
    head_count = lax.axis_size("heads")
    seq_pos = lax.axis_index("seq")
    head_pos = lax.axis_index("heads")
    first = (head_pos * heads).astype(jnp.int32).reshape(1)
    gains, shifts = ln_gain[0], ln_bias[0]
    part = rows // head_count

    own_docs = lax.dynamic_slice_in_dim(docs, seq_pos * rows, rows)
    lane = jnp.arange(LANES)[None, :]
    same = own_docs[:, None] == lane - DOC_LANE
    doc_lanes = (lane >= DOC_LANE) & (lane < DOC_LANE + DOCS)
    one_lanes = ((lane >= LSE_LANE) & (lane < LSE_LANE + 3)) | ((lane >= ONE_LANE) & (lane < ONE_LANE + 3))
    query_extra = (same & doc_lanes).astype(F32)
    pair_extra = jnp.where(doc_lanes & ~same, -BIG, one_lanes.astype(F32))

    w_three = jnp.transpose(w_qkv[0], (1, 0, 2))
    normed, queries, pairs = project(
        first, tokens, gains[0:1], shifts[0:1], w_three, b_qv[0], query_extra, pair_extra
    )
    distances = tuple(range(1, min(seq_count, STRIDE)))
    counts = jnp.asarray(count_columns(rows, max([0] + [group_of(item) for item in distances]) + 1))
    far = [flipped(pairs[:, : rows >> group_of(item)], item) for item in distances]
    outs, attn_part = attend(first, queries, pairs, far, distances, counts)

    w_out_all = lax.all_gather(w_out[0], "heads", axis=0, tiled=True)
    attn_all = lax.all_gather(attn_part, "heads", axis=1, tiled=True)
    current = tokens.astype(F32)
    resid = current + dot_nn(attn_all, w_out_all) + b_out[0]
    normed_two = norm_rows(resid, gains[1], shifts[1]).astype(BF16)
    pre = dot_nn(normed_two, w_up[0]) + b_up[0]
    share = 0.5 * (1.0 + lax.erf(pre * math.sqrt(0.5)))
    hidden = (pre * share).astype(BF16)
    slope = share + pre * jnp.exp(-0.5 * pre * pre) * (1.0 / math.sqrt(2.0 * math.pi))
    grad_pre = (dot_nt(cotangent, w_down[0]) * slope).astype(BF16)

    grad_two_part = lax.psum_scatter(
        dot_nt(grad_pre, w_up[0]).astype(BF16), "heads", scatter_dimension=0, tiled=True
    ).astype(F32)
    here = head_pos * part
    resid_part = lax.dynamic_slice_in_dim(resid, here, part)
    grad_out_part = lax.dynamic_slice_in_dim(cotangent, here, part).astype(F32)
    tokens_part = lax.dynamic_slice_in_dim(tokens, here, part).astype(F32)
    grad_resid_n, gain_two, shift_two = norm_back(resid_part, gains[1], grad_two_part)
    grad_resid = grad_out_part + grad_resid_n
    grad_resid_b = grad_resid.astype(BF16)
    grad_attn_part = dot_nt(grad_resid_b, w_out_all).astype(BF16)
    grad_attn = lax.all_to_all(
        grad_attn_part.reshape(part, head_count, feats), "heads", split_axis=1, concat_axis=0, tiled=True
    ).reshape(rows, feats)
    returned = attend_back(first, grad_attn, queries, pairs, outs, far, distances, counts)
    back = [flipped(item, distance) for item, distance in zip(returned[2:], distances)]
    grads_three = collect(first, returned[0], returned[1], back)

    out_sum = lax.psum_scatter(
        dot_nn(hidden, w_down[0]).astype(BF16), "heads", scatter_dimension=0, tiled=True
    ).astype(F32)
    out_part = (resid_part + out_sum + b_down[0]).astype(BF16)
    output = lax.all_gather(out_part, "heads", axis=0, tiled=True)

    grad_resid_all = lax.all_gather(grad_resid_b, "heads", axis=0, tiled=True)
    grad_w_out = dot_tn(attn_part, grad_resid_all)
    grad_w_up = dot_tn(normed_two, grad_pre)
    grad_w_down = dot_tn(hidden, cotangent)
    grad_w_qkv = jnp.stack([dot_tn(normed, item) for item in grads_three], axis=1)

    grad_one = functools.reduce(jnp.add, [dot_nt(item, w_three[index]) for index, item in enumerate(grads_three)])
    grad_one_part = lax.psum_scatter(grad_one.astype(BF16), "heads", scatter_dimension=0, tiled=True).astype(F32)
    grad_in_n, gain_one, shift_one = norm_back(tokens_part, gains[0], grad_one_part)
    grad_tokens = lax.all_gather((grad_resid + grad_in_n).astype(BF16), "heads", axis=0, tiled=True).astype(F32)

    wide_sums = lax.psum(
        jnp.stack(
            [gain_one, gain_two, shift_one, shift_two, jnp.sum(grad_resid, axis=0), jnp.sum(grad_out_part, axis=0)]
        ),
        ("seq", "heads"),
    )
    bias_sums = lax.psum(
        (
            jnp.stack([jnp.sum(item.astype(F32), axis=0) for item in (grads_three[0], grads_three[2])]),
            jnp.sum(grad_pre.astype(F32), axis=0),
        ),
        "seq",
    )
    weight_sums = lax.psum(
        tuple(item.astype(BF16) for item in (grad_w_up, grad_w_down, grad_w_out, grad_w_qkv)), "seq"
    )
    grad_w_up, grad_w_down, grad_w_out, grad_w_qkv = (item.astype(F32)[None] for item in weight_sums)
    return (
        output, grad_tokens, wide_sums[None, 0:2], wide_sums[None, 2:4], grad_w_qkv, bias_sums[0][None],
        grad_w_out, wide_sums[4:5], grad_w_up, bias_sums[1][None], grad_w_down, wide_sums[5:6],
    )


def solution(mesh):
    in_specs = (
        P("seq", None), P(), P(), P(), P(None, None, None, "heads"), P(None, None, "heads"),
        P(None, "heads", None), P(), P(None, None, "heads"), P(None, "heads"), P(None, "heads", None), P(),
        P("seq", None),
    )
    out_specs = (
        P("seq", None), P("seq", None), P(), P(), P(None, None, None, "heads"), P(None, None, "heads"),
        P(None, "heads", None), P(), P(None, None, "heads"), P(None, "heads"), P(None, "heads", None), P(),
    )
    return jax.shard_map(shards, mesh=mesh, in_specs=in_specs, out_specs=out_specs, check_vma=False)
```

time: 1180 us -> 512 us (0.43)
  waiting for transfers between devices: 536 us -> 227 us
  local copies, waits for them, and re-layouts: 272 us -> 39.2 us
  matrix products: 157 us -> 34.4 us
  other arithmetic: 140 us -> 29.4 us
  blocking collectives: 26.2 us -> 85.4 us
  Pallas kernels: 0 us -> 55.5 us
    psum x4 -> x1, waiting for transfers between devices: 525 us -> 74.9 us  [shards(): lax.psum(tuple((item.astype(BF16) for item in (grad_w_up, grad_w_down, gr...]
    mul x64 -> x0, local copies, waits for them, and re-layouts: 140 us -> none  [the longest x40 98.1 us: place_rows(): values[:, None] * pick_float[None, :, :, None]]
    dot_general x41 -> x15, matrix products: 153 us -> 34.4 us  [the longest x6 11.7 us: dot_nt(): lax.dot_general(left, right, (((1,), (1,)), ((), ())), preferred_element_...]
    reduce_scatter x0 -> x3, waiting for transfers between devices: none -> 72.3 us  [the longest x1 33.6 us: shards(): lax.psum_scatter(dot_nn(hidden, w_down[0]).astype(BF16), 'heads', scatter...]
    pallas_call x0 -> x4, Pallas kernels: none -> 55.5 us  [the longest x1 25.8 us: attend_back(): pl.pallas_call(functools.partial(attend_back_kernel, distances), grid=(he...]
    all_gather x0 -> x5, waiting for transfers between devices: none -> 51.9 us  [the longest x1 32.7 us: shards(): attn_all = lax.all_gather(attn_part, 'heads', axis=1, tiled=True)]
    unnamed x13 -> x3, other arithmetic: 39.6 us -> 2.59 us
    reduce_sum x24 -> x9, other arithmetic: 43.6 us -> 11.9 us  [the longest x1 3.43 us: shards(): jnp.sum(grad_resid, axis=0)]
  transfers between devices with their start and end apart: 40 -> 23, of which waited for: 9 -> 14; matrix products, arithmetic and copies ran while one was open for 36% -> 12% of each run, Pallas kernels for 0% -> 11%
where the time goes in v1:
time: 512 us; the launch traced here: 504 us
  waiting for transfers between devices  227 us (44%)
  blocking collectives  85.4 us (17%)
  Pallas kernels  55.5 us (11%)
  local copies, waits for them, and re-layouts  39.2 us (8%)
  matrix products  34.4 us (7%)
  other arithmetic  29.4 us (6%)
  starting transfers between devices  19.1 us (4%)
  between operations  14.8 us (3%)
    psum x1, waiting for transfers between devices, shards(): lax.psum(tuple((item.astype(BF16) for item in (grad_w_up, grad_w_down, gr...  74.9 us
    psum x1, blocking collectives, shards(): lax.psum(jnp.stack([gain_one, gain_two, shift_one, shift_two, jnp.sum(gra...  42.9 us
    reduce_scatter x1, waiting for transfers between devices, shards(): lax.psum_scatter(dot_nn(hidden, w_down[0]).astype(BF16), 'heads', scatter...  33.6 us
    all_gather x1, waiting for transfers between devices, shards(): attn_all = lax.all_gather(attn_part, 'heads', axis=1, tiled=True)  32.7 us
    unnamed x105, local copies, waits for them, and re-layouts  30.4 us
    all_to_all x1, blocking collectives, shards(): lax.all_to_all(grad_attn_part.reshape(part, head_count, feats), 'heads',...  27.8 us
    ppermute x14, waiting for transfers between devices, flipped(): lax.ppermute(array, 'seq', [(i, i ^ distance) for i in range(lax.axis_siz...  26.1 us
    pallas_call x1, Pallas kernels, attend_back(): pl.pallas_call(functools.partial(attend_back_kernel, distances), grid=(he...  25.8 us
  transfers between devices with their start and end apart: 23, of which 14 were waited for; matrix products, arithmetic and copies ran while one was open for 12% of the time, Pallas kernels for 11%

profile of v1, /device:TPU:0, one launch (start us, length us, event | category | flops | bytes accessed | tf_op | source)
XLA Modules:
  0.0 504.4 jit_solution(14069640013912118935)
XLA Ops:
  8.0 1.6 copy.59
  10.9 8.0 %project.1 = (bf16[1024,768]{1,0:T(8,128)(2,1)}, bf16[4,1024,128]{2,1,0:T(8,128)(2,1)S(1)}, bf16[4,1024,128]{2,1,0:T(8,128)(2,1)S(1)}) custom-call(s32[1]{0:T(128)} %bitcast.first_ref, bf16[1024,768]{1,0:T(8,128)(2,1)} %x_ref.1, f32[1,768]{1,0:T(1,128)S(1)} %get-tuple-element.106.gain_ref, f32[1,768]{1,0:T(1,128)S(1)} %get-tuple-element.108.shift_ref, ...), custom_call_target="tpu_custom_call" | custom-call | tf_op jit(solution)/shard_map/project/pallas_call | solution.py:150
  19.5 3.6 collective-permute-start.6
  23.2 1.4 collective-permute-start.2
  25.3 1.7 collective-permute-done.6.refs_6_
  27.0 2.3 collective-permute-start.4
  29.2 1.2 collective-permute-done.5.refs_5_
  30.5 1.8 collective-permute-start.3
  33.0 3.1 collective-permute-done.3.refs_3_
  36.1 5.3 %collective-permute-done.1.refs_1_ = bf16[4,256,128]{2,1,0:T(8,128)(2,1)S(1)} collective-permute-done((bf16[4,256,128]{2,1,0:T(8,128)(2,1)S(1)}, bf16[4,256,128]{2,1,0:T(8,128)(2,1)S(1)}, u32[]{:S(2)}, u32[]{:S(2)}) %collective-permute-start.1) | collective-permute-done | bytes 262176 | tf_op jit(solution)/shard_map/ppermute | solution.py:385
  41.4 16.0 %attend.1 = (f32[4,1024,128]{2,1,0:T(8,128)}, bf16[1024,192]{1,0:T(8,128)(2,1)S(1)}) custom-call(s32[1]{0:T(128)} %bitcast.first_ref, bf16[4,1024,128]{2,1,0:T(8,128)(2,1)S(1)} %get-tuple-element.29.q_ref, bf16[4,1024,128]{2,1,0:T(8,128)(2,1)S(1)} %get-tuple-element.30.kv_ref, bf16[4,1024,128]{2,1,0:T(8,128)(2,1)S(1)} %copy-done.3, ...), custom_call_target="tpu_custom_call" | custom-call | tf_op jit(solution)/shard_map/attend/pallas_call | solution.py:226
  58.2 2.0 copy.60
  60.4 2.6 copy.58
  63.7 1.3 reduce
  65.0 32.7 %all-gather.7.cloned.1.call-done = bf16[1024,768]{0,1:T(8,128)(2,1)} async-done(((bf16[1024,192]{0,1:T(8,128)(2,1)}), bf16[1024,768]{0,1:T(8,128)(2,1)}) %all-gather.7.cloned.1.call-update) | async-done | bytes 1572880 | tf_op jit(solution)/shard_map/all_gather | solution.py:418
  97.7 3.9 fusion.47
  102.0 1.2 copy-done.33
  104.6 3.2 multiply_convert_fusion
  107.8 3.4 convert_reduce_fusion
  111.2 1.2 copy-done.49
  112.4 2.6 convolution_convert_fusion
  115.0 4.4 convolution_convert_fusion.1
  121.5 1.9 copy.77
  123.4 1.2 dynamic-slice_reduce_fusion
  125.3 1.3 multiply_reduce_fusion.1
  127.1 22.2 %reduce-scatter.6.cloned.1.call-done = bf16[256,768]{0,1:T(8,128)(2,1)} async-done(((bf16[1024,768]{0,1:T(8,128)(2,1)}), bf16[256,768]{0,1:T(8,128)(2,1)}) %reduce-scatter.6.cloned.1.call-update) | async-done | bytes 393232 | tf_op jit(solution)/shard_map/reduce_scatter | solution.py:428
  149.3 1.7 fusion.37
  152.1 33.6 %reduce-scatter.4.cloned.1.call-done = bf16[256,768]{0,1:T(8,128)(2,1)} async-done(((bf16[1024,768]{0,1:T(8,128)(2,1)}), bf16[256,768]{0,1:T(8,128)(2,1)}) %reduce-scatter.4.cloned.1.call-update) | async-done | bytes 393232 | tf_op jit(solution)/shard_map/reduce_scatter | solution.py:446
  185.7 3.4 fusion.45
  190.9 2.7 convolution_convert_fusion.4
  193.6 1.9 copy.65
  195.5 27.8 %all_to_all.15 = bf16[256,4,192]{0,2,1:T(8,128)(2,1)} all-to-all(bf16[256,4,192]{0,2,1:T(8,128)(2,1)} %bitcast.95), channel_id=1, replica_groups=mesh['seq'=8,'heads'=4] {'heads'}, dimensions={1} | all-to-all | bytes 786432 | tf_op jit(solution)/shard_map/all_to_all | solution.py:439
  223.3 2.0 copy.66
  225.3 1.2 copy-done.2
  226.6 1.2 copy-done.5
  235.3 25.8 %attend_back.1 = (f32[4,1024,128]{2,1,0:T(8,128)}, f32[4,1024,128]{2,1,0:T(8,128)}, bf16[4,512,128]{2,1,0:T(8,128)(2,1)S(1)}, bf16[4,256,128]{2,1,0:T(8,128)(2,1...) custom-call(s32[1]{0:T(128)} %bitcast.first_ref, ...), custom_call_target="tpu_custom_call" | custom-call | tf_op jit(solution)/shard_map/attend_back/pallas_call | solution.py:306
  261.2 1.5 collective-permute-start.10
  263.0 1.5 collective-permute-start.8
  264.7 2.8 collective-permute-done.10.refs_3_
  267.5 2.4 collective-permute-start.12
  269.8 2.1 collective-permute-start.13
  271.9 9.5 %collective-permute-done.12.refs_5_ = bf16[4,128,128]{2,1,0:T(8,128)(2,1)S(1)} collective-permute-done((bf16[4,128,128]{2,1,0:T(8,128)(2,1)S(1)}, bf16[4,128,128]{2,1,0:T(8,128)(2,1)S(1)}, u32[]{:S(2)}, u32[]{:S(2)}) %collective-permute-start.12) | collective-permute-done | bytes 131104 | tf_op jit(solution)/shard_map/ppermute | solution.py:385
  281.4 1.7 collective-permute-done.13.refs_6_
  283.1 1.6 copy-done.6
  284.7 5.7 %collect.1 = (bf16[1024,192]{1,0:T(8,128)(2,1)S(1)}, bf16[1024,192]{1,0:T(8,128)(2,1)S(1)}, bf16[1024,192]{1,0:T(8,128)(2,1)S(1)}) custom-call(s32[1]{0:T(128)} %bitcast.first_ref, f32[4,1024,128]{2,1,0:T(8,128)S(1)} %copy-done.6, f32[4,1024,128]{2,1,0:T(8,128)} %get-tuple-element.34.dkv_ref, bf16[512,192]{1,0:T(8,128)(2,1)S(1)} %copy-done.29, ...), custom_call_target="tpu_custom_call" | custom-call | tf_op jit(solution)/shard_map/collect/pallas_call | solution.py:371
  292.0 1.8 add_convert_fusion
  295.0 4.4 fusion.6
  299.4 2.5 fusion.7
  305.1 2.8 fusion.18
  308.0 1.1 convert_reduce_fusion.5
  309.1 1.2 fusion.32
  310.3 16.5 %reduce-scatter.8.cloned.1.call-done = bf16[256,768]{0,1:T(8,128)(2,1)} async-done(((bf16[1024,768]{0,1:T(8,128)(2,1)}), bf16[256,768]{0,1:T(8,128)(2,1)}) %reduce-scatter.8.cloned.1.call-update) | async-done | bytes 393232 | tf_op jit(solution)/shard_map/reduce_scatter | solution.py:459
  326.8 1.6 fusion.38
  328.5 2.4 fusion.31
  331.3 14.6 %all-reduce = (f32[1,2,192]{2,1,0:T(2,128)}, f32[1,768]{1,0:T(1,128)}) all-reduce(f32[1,2,192]{2,1,0:T(2,128)S(1)} %maximum_bitcast_fusion.1, f32[1,768]{1,0:T(1,128)S(1)} %broadcast_in_dim.71), channel_id=1, replica_groups=mesh['seq'=8,'heads'=4] {'seq'}, use_global_device_ids=true, to_apply=%region_23.24 | all-reduce | flops 1152 | bytes 9216 | tf_op jit(solution)/shard_map/psum | solution.py:469
  345.9 19.1 %all-gather.9.cloned.1.call-done = bf16[1024,768]{0,1:T(8,128)(2,1)} async-done(((bf16[256,768]{0,1:T(8,128)(2,1)}), bf16[1024,768]{0,1:T(8,128)(2,1)}) %all-gather.9.cloned.1.call-update) | async-done | bytes 1572880 | tf_op jit(solution)/shard_map/all_gather | solution.py:450
  365.1 2.6 copy.70
  367.7 74.9 %all-reduce.4.cloned.1.call-done = (bf16[1,768,3,192]{1,3,2,0:T(8,128)(2,1)}, bf16[1,192,768]{2,1,0:T(8,128)(2,1)}, bf16[1,768,768]{2,1,0:T(8,128)(2,1)}, bf16[1,768,768]{2,1,0:T(8,128)(2,1)}) async-done(((bf16[1,768,3,192]{1,3,2,0:T(8,128)(2,1)}, bf16[1,192,768]{2,1,0:T(8,128)(2,1)}, bf16[1,768,768]{2,1,0:T(8,128)(2,1)}, bf16[1,768,768]{2,1,0:T(8,128)(2,1)}), (bf16[1,768,3,192]{1,3,2,0:T(8,128)(2,1)}, ...) | async-done | bytes 3538960 | tf_op jit(solution)/shard_map/psum | solution.py:476
  442.6 1.9 broadcast_in_dim.68
  444.5 2.5 broadcast_in_dim.65
  447.0 1.6 broadcast_in_dim.70
  448.7 1.6 broadcast_in_dim.73
  450.3 42.9 %psum.49 = f32[6,768]{1,0:T(8,128)S(1)} all-reduce(f32[6,768]{1,0:T(8,128)S(1)} %stack.52), channel_id=1, replica_groups=mesh['seq'=8,'heads'=4] {'seq','heads'}, use_global_device_ids=true, to_apply=%region_19.20 | all-reduce | flops 4608 | bytes 36864 | tf_op jit(solution)/shard_map/psum | solution.py:463
  494.4 3.1 copy.71
  (174 shorter events, 29.4 us)
Async XLA Ops:
  7.2 100.6 %copy-start = (bf16[1024,768]{1,0:T(8,128)(2,1)S(1)}, bf16[1024,768]{1,0:T(8,128)(2,1)}, u32[]{:S(2)}) copy-start(bf16[1024,768]{1,0:T(8,128)(2,1)} %param.33) | copy-start | bytes 4718596
  7.2 3.2 copy-start.42
  7.2 3.2 copy-start.41
  7.2 57.8 %all-gather.15.cloned.1.call-start = ((), (), s32[]{:S(2)}) async-start(), calls=%async_computation.11 | async-start | bytes 1474560 | tf_op jit(solution)/shard_map/all_gather | solution.py:417
  7.9 89.8 %all-gather.7.cloned.1.call-start = ((), (), s32[]{:S(2)}) async-start(), calls=%async_computation.4 | async-start | bytes 1966080 | tf_op jit(solution)/shard_map/all_gather | solution.py:418
  8.0 2.8 copy-start.17
  8.0 2.8 copy-start.30
  8.0 2.8 copy-start.31
  8.0 2.8 copy-start.32
  18.9 38.4 %copy-start.1 = (bf16[4,1024,128]{2,1,0:T(8,128)(2,1)}, bf16[4,1024,128]{2,1,0:T(8,128)(2,1)S(1)}, u32[]{:S(2)}) copy-start(bf16[4,1024,128]{2,1,0:T(8,128)(2,1)S(1)} %get-tuple-element.30.kv_ref) | copy-start | bytes 3145732
  18.9 38.4 %copy-start.4 = (bf16[4,1024,128]{2,1,0:T(8,128)(2,1)}, bf16[4,1024,128]{2,1,0:T(8,128)(2,1)S(1)}, u32[]{:S(2)}) copy-start(bf16[4,1024,128]{2,1,0:T(8,128)(2,1)S(1)} %get-tuple-element.29.q_ref) | copy-start | bytes 3145732
  18.9 22.5 %copy-start.3 = (bf16[4,1024,128]{2,1,0:T(8,128)(2,1)S(1)}, bf16[4,1024,128]{2,1,0:T(8,128)(2,1)}, u32[]{:S(2)}) copy-start(bf16[4,1024,128]{2,1,0:T(8,128)(2,1)} %constant.78.clone.count_ref) | copy-start | bytes 3145732
  18.9 22.5 %copy-start.12 = (bf16[512,192]{1,0:T(8,128)(2,1)S(1)}, bf16[512,192]{1,0:T(8,128)(2,1)}, u32[]{:S(2)}) copy-start(bf16[512,192]{1,0:T(8,128)(2,1)} %constant.79.clone.gather_ref.gather_v_ref) | copy-start | bytes 589828
  19.0 22.4 %collective-permute-start = (bf16[4,512,128]{2,1,0:T(8,128)(2,1)S(1)}, bf16[4,512,128]{2,1,0:T(8,128)(2,1)S(1)}, u32[]{:S(2)}, u32[]{:S(2)}) collective-permute-start(bf16[4,512,128]{2,1,0:T(8,128)(2,1)S(1)} %slice.60), channel_id=1, source_target_pairs={{0,4},{4,0},{8,12},{12,8},{16,20},{20,16},{24,28},{28,24},{1,5},{5... | collective-permute-start | bytes 1572872 | tf_op jit(solution)/shard_map/ppermute | solution.py:385
  19.5 7.5 %collective-permute-start.6 = (bf16[4,128,128]{2,1,0:T(8,128)(2,1)S(1)}, bf16[4,128,128]{2,1,0:T(8,128)(2,1)S(1)}, u32[]{:S(2)}, u32[]{:S(2)}) collective-permute-start(bf16[4,128,128]{2,1,0:T(8,128)(2,1)S(1)} %slice.62), channel_id=1, source_target_pairs={{0,28},{4,24},{8,20},{12,16},{16,12},{20,8},{24,4},{28,0},{1,29},{... | collective-permute-start | bytes 393224 | tf_op jit(solution)/shard_map/ppermute | solution.py:385
  23.1 7.3 %collective-permute-start.5 = (bf16[4,128,128]{2,1,0:T(8,128)(2,1)S(1)}, bf16[4,128,128]{2,1,0:T(8,128)(2,1)S(1)}, u32[]{:S(2)}, u32[]{:S(2)}) collective-permute-start(bf16[4,128,128]{2,1,0:T(8,128)(2,1)S(1)} %slice.62), channel_id=1, source_target_pairs={{0,24},{4,28},{8,16},{12,20},{16,8},{20,12},{24,0},{28,4},{1,25},{... | collective-permute-start | bytes 393224 | tf_op jit(solution)/shard_map/ppermute | solution.py:385
  23.2 12.9 %collective-permute-start.2 = (bf16[4,256,128]{2,1,0:T(8,128)(2,1)S(1)}, bf16[4,256,128]{2,1,0:T(8,128)(2,1)S(1)}, u32[]{:S(2)}, u32[]{:S(2)}) collective-permute-start(bf16[4,256,128]{2,1,0:T(8,128)(2,1)S(1)} %slice.61), channel_id=1, source_target_pairs={{0,12},{4,8},{8,4},{12,0},{16,28},{20,24},{24,20},{28,16},{1,13},{... | collective-permute-start | bytes 786440 | tf_op jit(solution)/shard_map/ppermute | solution.py:385
  24.5 16.9 %collective-permute-start.1 = (bf16[4,256,128]{2,1,0:T(8,128)(2,1)S(1)}, bf16[4,256,128]{2,1,0:T(8,128)(2,1)S(1)}, u32[]{:S(2)}, u32[]{:S(2)}) collective-permute-start(bf16[4,256,128]{2,1,0:T(8,128)(2,1)S(1)} %slice.61), channel_id=1, source_target_pairs={{0,8},{4,12},{8,0},{12,4},{16,24},{20,28},{24,16},{28,20},{1,9},{5... | collective-permute-start | bytes 786440 | tf_op jit(solution)/shard_map/ppermute | solution.py:385
  27.0 30.4 %copy-start.19 = (bf16[4,128,128]{2,1,0:T(8,128)(2,1)}, bf16[4,128,128]{2,1,0:T(8,128)(2,1)S(1)}, u32[]{:S(2)}) copy-start(bf16[4,128,128]{2,1,0:T(8,128)(2,1)S(1)} %collective-permute-done.6.refs_6_) | copy-start | bytes 393220
  27.0 6.0 %collective-permute-start.4 = (bf16[4,128,128]{2,1,0:T(8,128)(2,1)S(1)}, bf16[4,128,128]{2,1,0:T(8,128)(2,1)S(1)}, u32[]{:S(2)}, u32[]{:S(2)}) collective-permute-start(bf16[4,128,128]{2,1,0:T(8,128)(2,1)S(1)} %slice.62), channel_id=1, source_target_pairs={{0,20},{4,16},{8,28},{12,24},{16,4},{20,0},{24,12},{28,8},{1,21},{... | collective-permute-start | bytes 393224 | tf_op jit(solution)/shard_map/ppermute | solution.py:385
  30.5 26.9 %copy-start.21 = (bf16[4,128,128]{2,1,0:T(8,128)(2,1)}, bf16[4,128,128]{2,1,0:T(8,128)(2,1)S(1)}, u32[]{:S(2)}) copy-start(bf16[4,128,128]{2,1,0:T(8,128)(2,1)S(1)} %collective-permute-done.5.refs_5_) | copy-start | bytes 393220
  30.5 5.6 %collective-permute-start.3 = (bf16[4,128,128]{2,1,0:T(8,128)(2,1)S(1)}, bf16[4,128,128]{2,1,0:T(8,128)(2,1)S(1)}, u32[]{:S(2)}, u32[]{:S(2)}) collective-permute-start(bf16[4,128,128]{2,1,0:T(8,128)(2,1)S(1)} %slice.62), channel_id=1, source_target_pairs={{0,16},{4,20},{8,24},{12,28},{16,0},{20,4},{24,8},{28,12},{1,17},{... | collective-permute-start | bytes 393224 | tf_op jit(solution)/shard_map/ppermute | solution.py:385
  33.0 24.4 %copy-start.23 = (bf16[4,128,128]{2,1,0:T(8,128)(2,1)}, bf16[4,128,128]{2,1,0:T(8,128)(2,1)S(1)}, u32[]{:S(2)}) copy-start(bf16[4,128,128]{2,1,0:T(8,128)(2,1)S(1)} %collective-permute-done.4.refs_4_) | copy-start | bytes 393220
  36.1 21.3 %copy-start.25 = (bf16[4,128,128]{2,1,0:T(8,128)(2,1)}, bf16[4,128,128]{2,1,0:T(8,128)(2,1)S(1)}, u32[]{:S(2)}) copy-start(bf16[4,128,128]{2,1,0:T(8,128)(2,1)S(1)} %collective-permute-done.3.refs_3_) | copy-start | bytes 393220
  36.1 21.3 %copy-start.13 = (bf16[4,256,128]{2,1,0:T(8,128)(2,1)}, bf16[4,256,128]{2,1,0:T(8,128)(2,1)S(1)}, u32[]{:S(2)}) copy-start(bf16[4,256,128]{2,1,0:T(8,128)(2,1)S(1)} %collective-permute-done.2.refs_2_) | copy-start | bytes 786436
  41.4 16.0 %copy-start.15 = (bf16[4,256,128]{2,1,0:T(8,128)(2,1)}, bf16[4,256,128]{2,1,0:T(8,128)(2,1)S(1)}, u32[]{:S(2)}) copy-start(bf16[4,256,128]{2,1,0:T(8,128)(2,1)S(1)} %collective-permute-done.1.refs_1_) | copy-start | bytes 786436
  60.2 89.0 %reduce-scatter.6.cloned.1.call-start = ((), (), s32[]{:S(2)}) async-start(), calls=%async_computation.7 | async-start | bytes 1966080 | tf_op jit(solution)/shard_map/reduce_scatter | solution.py:428
  101.6 1.7 copy-start.33
  103.3 1.3 copy-start.46
  104.6 3.2 copy-start.35
  104.6 3.2 copy-start.47
  111.2 1.2 copy-start.49
  115.0 70.7 %reduce-scatter.4.cloned.1.call-start = ((), (), s32[]{:S(2)}) async-start(), calls=%async_computation.5 | async-start | bytes 1966080 | tf_op jit(solution)/shard_map/reduce_scatter | solution.py:446
  119.4 185.6 %all-gather.13.cloned.1.call-start = ((), (), s32[]{:S(2)}) async-start(), calls=%async_computation.10 | async-start | bytes 1966080 | tf_op jit(solution)/shard_map/all_gather | solution.py:452
  190.9 136.0 %reduce-scatter.8.cloned.1.call-start = ((), (), s32[]{:S(2)}) async-start(), calls=%async_computation.8 | async-start | bytes 1966080 | tf_op jit(solution)/shard_map/reduce_scatter | solution.py:459
  225.3 1.2 copy-start.2
  226.6 1.2 copy-start.5
  227.8 1.0 copy-start.7
  228.8 1.0 copy-start.14
  229.8 0.9 copy-start.16
  230.7 0.9 copy-start.18
  235.3 47.8 %copy-start.29 = (bf16[512,192]{1,0:T(8,128)(2,1)S(1)}, bf16[512,192]{1,0:T(8,128)(2,1)}, u32[]{:S(2)}) copy-start(bf16[512,192]{1,0:T(8,128)(2,1)} %constant.80.clone.gather_k_ref) | copy-start | bytes 589828
  261.1 22.0 %collective-permute-start.7 = (bf16[4,512,128]{2,1,0:T(8,128)(2,1)S(1)}, bf16[4,512,128]{2,1,0:T(8,128)(2,1)S(1)}, u32[]{:S(2)}, u32[]{:S(2)}) collective-permute-start(bf16[4,512,128]{2,1,0:T(8,128)(2,1)S(1)} %get-tuple-element.35), channel_id=1, source_target_pairs={{0,4},{4,0},{8,12},{12,8},{16,20},{20,16},{24,28},{28,24},{1,5},{5... | collective-permute-start | bytes 1572872 | tf_op jit(solution)/shard_map/ppermute | solution.py:385
  261.2 6.3 %collective-permute-start.10 = (bf16[4,128,128]{2,1,0:T(8,128)(2,1)S(1)}, bf16[4,128,128]{2,1,0:T(8,128)(2,1)S(1)}, u32[]{:S(2)}, u32[]{:S(2)}) collective-permute-start(bf16[4,128,128]{2,1,0:T(8,128)(2,1)S(1)} %get-tuple-element.38), channel_id=1, source_target_pairs={{0,16},{4,20},{8,24},{12,28},{16,0},{20,4},{24,8},{28,12},{1,17},{... | collective-permute-start | bytes 393224 | tf_op jit(solution)/shard_map/ppermute | solution.py:385
  262.6 7.2 %collective-permute-start.11 = (bf16[4,128,128]{2,1,0:T(8,128)(2,1)S(1)}, bf16[4,128,128]{2,1,0:T(8,128)(2,1)S(1)}, u32[]{:S(2)}, u32[]{:S(2)}) collective-permute-start(bf16[4,128,128]{2,1,0:T(8,128)(2,1)S(1)} %get-tuple-element.39), channel_id=1, source_target_pairs={{0,20},{4,16},{8,28},{12,24},{16,4},{20,0},{24,12},{28,8},{1,21},{... | collective-permute-start | bytes 393224 | tf_op jit(solution)/shard_map/ppermute | solution.py:385
  263.0 20.1 %collective-permute-start.8 = (bf16[4,256,128]{2,1,0:T(8,128)(2,1)S(1)}, bf16[4,256,128]{2,1,0:T(8,128)(2,1)S(1)}, u32[]{:S(2)}, u32[]{:S(2)}) collective-permute-start(bf16[4,256,128]{2,1,0:T(8,128)(2,1)S(1)} %get-tuple-element.36), channel_id=1, source_target_pairs={{0,8},{4,12},{8,0},{12,4},{16,24},{20,28},{24,16},{28,20},{1,9},{5... | collective-permute-start | bytes 786440 | tf_op jit(solution)/shard_map/ppermute | solution.py:385
  264.4 18.7 %collective-permute-start.9 = (bf16[4,256,128]{2,1,0:T(8,128)(2,1)S(1)}, bf16[4,256,128]{2,1,0:T(8,128)(2,1)S(1)}, u32[]{:S(2)}, u32[]{:S(2)}) collective-permute-start(bf16[4,256,128]{2,1,0:T(8,128)(2,1)S(1)} %get-tuple-element.37), channel_id=1, source_target_pairs={{0,12},{4,8},{8,4},{12,0},{16,28},{20,24},{24,20},{28,16},{1,13},{... | collective-permute-start | bytes 786440 | tf_op jit(solution)/shard_map/ppermute | solution.py:385
  267.5 14.0 %collective-permute-start.12 = (bf16[4,128,128]{2,1,0:T(8,128)(2,1)S(1)}, bf16[4,128,128]{2,1,0:T(8,128)(2,1)S(1)}, u32[]{:S(2)}, u32[]{:S(2)}) collective-permute-start(bf16[4,128,128]{2,1,0:T(8,128)(2,1)S(1)} %get-tuple-element.40), channel_id=1, source_target_pairs={{0,24},{4,28},{8,16},{12,20},{16,8},{20,12},{24,0},{28,4},{1,25},{... | collective-permute-start | bytes 393224 | tf_op jit(solution)/shard_map/ppermute | solution.py:385
  269.8 13.2 %collective-permute-start.13 = (bf16[4,128,128]{2,1,0:T(8,128)(2,1)S(1)}, bf16[4,128,128]{2,1,0:T(8,128)(2,1)S(1)}, u32[]{:S(2)}, u32[]{:S(2)}) collective-permute-start(bf16[4,128,128]{2,1,0:T(8,128)(2,1)S(1)} %get-tuple-element.41), channel_id=1, source_target_pairs={{0,28},{4,24},{8,20},{12,16},{16,12},{20,8},{24,4},{28,0},{1,29},{... | collective-permute-start | bytes 393224 | tf_op jit(solution)/shard_map/ppermute | solution.py:385
  283.1 1.6 copy-start.6
  290.4 1.0 copy-start.27
  293.9 71.2 %all-gather.9.cloned.1.call-start = ((), (), s32[]{:S(2)}) async-start(), calls=%async_computation.6 | async-start | bytes 1966080 | tf_op jit(solution)/shard_map/all_gather | solution.py:450
  294.7 147.9 %all-reduce.4.cloned.1.call-start = ((), (), s32[]{:S(2)}) async-start(), calls=%async_computation.12 | async-start | bytes 7077888 | tf_op jit(solution)/shard_map/psum | solution.py:476
  295.0 4.4 copy-start.48
  299.4 2.5 copy-start.28
  299.4 2.5 copy-start.45
  301.9 1.0 copy-start.11
  304.0 1.1 copy-start.9
  307.9 186.4 %all-gather.11.cloned.1.call-start = ((), (), s32[]{:S(2)}) async-start(), calls=%async_computation.9 | async-start | bytes 1966080 | tf_op jit(solution)/shard_map/all_gather | solution.py:461
  326.8 4.1 copy-start.43
  326.8 4.1 copy-start.39
  326.8 4.1 copy-start.38
  442.6 4.4 copy-start.37
  447.0 1.7 copy-start.36
  (9 other events, 7.4 us)
Sparse Core Ops, SparseCore 0:
  9.6 33.1 all-gather.14
  60.3 37.3 all-gather.6
  115.1 34.1 reduce-scatter.5
  151.4 34.2 reduce-scatter.3
  191.0 46.4 all-gather.12
  294.0 32.7 reduce-scatter.7
  328.4 36.6 all-gather.8
  369.9 72.6 all-reduce.3
  444.1 38.7 all-gather.10
